TPU v7x, 128 devices: a whole 4x4x4 slice. The times are simulated.
128 devices in a mesh: row: 8 (over x, z_hi), col: 16 (over y, z_lo, core).
Axes of the slice: x: 4, y: 4, z: 4 (z_hi: 2, z_lo: 2; z = z_hi * 2 + z_lo), core: 2. Of those that a mesh axis runs over, the one named last changes fastest.
Arguments:
- residual: bfloat16 [256, 5120], P('row', 'col'), may hold values from -6 to 6
- attn_gain: float32 [5120], P('col'), may hold values from 0.1 to 1.9
- w_query: bfloat16 [5120, 5120], P('col', 'row'), may hold values from -0.078125 to 0.078125
- w_key: bfloat16 [5120, 1024], P('col', 'row'), may hold values from -0.078125 to 0.078125
- w_value: bfloat16 [5120, 1024], P('col', 'row'), may hold values from -0.078125 to 0.078125
- w_out: bfloat16 [5120, 5120], P('row', 'col'), may hold values from -0.078125 to 0.078125
- mlp_gain: float32 [5120], P('col'), may hold values from 0.1 to 1.9
- w_gate: bfloat16 [2, 5120, 13824], P(None, 'col', 'row'), may hold values from -0.078125 to 0.078125
- w_up: bfloat16 [2, 5120, 13824], P(None, 'col', 'row'), may hold values from -0.078125 to 0.078125
- w_down: bfloat16 [2, 13824, 5120], P(None, 'row', 'col'), may hold values from -0.0546875 to 0.0546875
- final_gain: float32 [5120], P('col'), may hold values from 0.1 to 1.9
- w_head: bfloat16 [5120, 81920], P(None, ('row', 'col')), may hold values from -32 to 32
- seq_lengths: int32 [8], replicated, may hold values from 1 to 64, 256 in all
- targets: int32 [256], replicated, may hold values from 0 to 81919
Outputs:
- seq_diff: float32 [8], replicated
Inputs may be any that keep to these rules, and one draw needn't show every extreme that they name: `seq_lengths`: the lengths sum to 256 and the largest is exactly 64.
All inputs are finite; a program needn't handle non-finite values.
Results may differ from a plain program's by a relative error of at most 0.02.
Values may be sent and summed in bfloat16 or wider, within the bound.
A program may use at most 64 MiB of HBM per device.

v0:
```python
import jax
import jax.numpy as jnp
from jax import lax
from jax.sharding import PartitionSpec as P

D = 5120
HEAD_DIM = 128
SEQS = 8


EPSILON = 1e-06
ROPE_BASE = 1000000.0
MASKED = -1e30


def sequence_layout(seq_lengths, token_index):
    ends_at = jnp.cumsum(seq_lengths)
    before = ends_at[None, :] <= token_index[:, None]
    segment = jnp.sum(before.astype(jnp.int32), axis=1)
    starts_at = jnp.sum(jnp.where(before, seq_lengths[None, :], 0), axis=1)
    return (segment, (token_index - starts_at).astype(jnp.float32))


def angles_for(positions, head_width):
    exponent = jnp.arange(head_width // 2, dtype=jnp.float32) * 2.0 / head_width
    frequency = ROPE_BASE ** (-exponent)
    return positions[:, None] * frequency[None, :]


def rotate(features, angles):
    half_width = features.shape[-1] // 2
    lower_half = features[..., :half_width]
    upper_half = features[..., half_width:]
    cosine = jnp.cos(angles)[:, None, :]
    sine_part = jnp.sin(angles)[:, None, :]
    return jnp.concatenate(
        [
            lower_half * cosine - upper_half * sine_part,
            upper_half * cosine + lower_half * sine_part,
        ],
        axis=-1,
    )


def rms_local(features, gain_vector):
    squares = jnp.sum(features * features, axis=1)
    grand_total = lax.psum(squares, "col")
    return features * lax.rsqrt(grand_total / D + EPSILON)[:, None] * gain_vector[None, :]


def feed_forward(mlp_input, gate_up, down_weight):
    ff_local = down_weight.shape[0]
    row_block = mlp_input
    summed = lax.psum_scatter(
        jnp.dot(row_block, gate_up, preferred_element_type=jnp.float32),
        "col",
        scatter_dimension=0,
        tiled=True,
    )
    hidden = (jax.nn.silu(summed[:, :ff_local]) * summed[:, ff_local:]).astype(jnp.bfloat16)
    hidden_all = lax.all_gather(hidden, "col", axis=0, tiled=True)
    row_block = hidden_all
    return lax.psum_scatter(
        jnp.dot(row_block, down_weight, preferred_element_type=jnp.float32),
        "row",
        scatter_dimension=0,
        tiled=True,
    )


def per_device(
    residual,
    attn_gain,
    w_query,
    w_key,
    w_value,
    w_out,
    mlp_gain,
    w_gate,
    w_up,
    w_down,
    final_gain,
    w_head,
    seq_lengths,
    targets,
):
    row_count = lax.axis_size("row")
    col_count = lax.axis_size("col")
    row_index = lax.axis_index("row")
    col_index = lax.axis_index("col")
    local_rows = residual.shape[0]
    total_tokens = local_rows * row_count
    query_heads = w_query.shape[1] // HEAD_DIM
    kv_local = w_key.shape[1] // HEAD_DIM
    group_size = query_heads // kv_local
    query_width = query_heads * HEAD_DIM
    key_width = kv_local * HEAD_DIM
    stream_in = residual.astype(jnp.float32)
    normed = rms_local(stream_in, attn_gain).astype(jnp.bfloat16)
    gathered = lax.all_gather(normed, "row", axis=0, tiled=True)
    w_joint = jnp.concatenate([w_query, w_key, w_value], axis=1)
    joint_part = jnp.dot(gathered, w_joint, preferred_element_type=jnp.float32)
    joint_sums = lax.psum(joint_part, "col")
    token_index = jnp.arange(total_tokens, dtype=jnp.int32)
    segment, positions = sequence_layout(seq_lengths, token_index)
    angles = angles_for(positions, HEAD_DIM)
    queries = rotate(
        joint_sums[:, :query_width].reshape(total_tokens, query_heads, HEAD_DIM), angles
    ).astype(jnp.bfloat16)
    keys_all = rotate(
        joint_sums[:, query_width : query_width + key_width].reshape(
            total_tokens, kv_local, HEAD_DIM
        ),
        angles,
    ).astype(jnp.bfloat16)
    values_all = (
        joint_sums[:, query_width + key_width :]
        .astype(jnp.bfloat16)
        .reshape(total_tokens, kv_local, HEAD_DIM)
    )
    grouped = queries.reshape(total_tokens, kv_local, group_size, HEAD_DIM)
    block_rows = min(512, total_tokens)
    block_count = total_tokens // block_rows

    def attend_block(block_start):
        block_index = block_start + jnp.arange(block_rows, dtype=jnp.int32)
        scores = jnp.einsum(
            "qhgd,khd->hgqk", grouped, keys_all, preferred_element_type=jnp.float32
        ) * HEAD_DIM ** (-0.5)
        allowed = (segment[:, None] == segment[None, :]) & (
            token_index[None, :] <= block_index[:, None]
        )
        scores = jnp.where(allowed[None, None], scores, MASKED)
        top_value = jnp.max(scores, axis=-1, keepdims=True)
        weights = jnp.exp(scores - top_value)
        weights = (weights / jnp.sum(weights, axis=-1, keepdims=True)).astype(jnp.bfloat16)
        result = jnp.einsum(
            "hgqk,khd->qhgd", weights, values_all, preferred_element_type=jnp.float32
        )
        return result.astype(jnp.bfloat16).reshape(block_rows, query_width)

    block_starts = jnp.arange(block_count, dtype=jnp.int32) * block_rows
    attn_all = lax.map(attend_block, block_starts).reshape(total_tokens, query_width)
    projected = lax.psum_scatter(
        jnp.dot(attn_all, w_out, preferred_element_type=jnp.float32),
        "row",
        scatter_dimension=0,
        tiled=True,
    )
    stream = lax.optimization_barrier((stream_in + projected).astype(jnp.bfloat16))
    stream_f = stream.astype(jnp.float32)
    mlp_in = rms_local(stream_f, mlp_gain).astype(jnp.bfloat16)
    mlp_input = lax.all_gather(mlp_in, "row", axis=0, tiled=True)
    outputs = []
    for member in range(2):
        gate_up = jnp.concatenate([w_gate[member], w_up[member]], axis=1)
        outputs.append(stream_f + feed_forward(mlp_input, gate_up, w_down[member]))
    pair_sums = lax.psum(
        (jnp.sum(outputs[0] * outputs[0], axis=1), jnp.sum(outputs[1] * outputs[1], axis=1)), "col"
    )
    policy_final = (
        outputs[0] * lax.rsqrt(pair_sums[0] / D + EPSILON)[:, None] * final_gain[None, :]
    ).astype(jnp.bfloat16)
    refer_final = (
        outputs[1] * lax.rsqrt(pair_sums[1] / D + EPSILON)[:, None] * final_gain[None, :]
    ).astype(jnp.bfloat16)
    wide_pair = (
        lax.all_gather(policy_final, "col", axis=1, tiled=True),
        lax.all_gather(refer_final, "col", axis=1, tiled=True),
    )
    policy_all, refer_all = (
        lax.all_gather(wide_pair[0], "row", axis=0, tiled=True),
        lax.all_gather(wide_pair[1], "row", axis=0, tiled=True),
    )
    vocab_local = w_head.shape[1]
    vocab_start = (row_index * col_count + col_index) * vocab_local
    vocab_ids = vocab_start + jnp.arange(vocab_local, dtype=jnp.int32)
    target_hits = targets[:, None] == vocab_ids[None, :]

    def local_stats(final_all):
        logits = jnp.dot(final_all, w_head, preferred_element_type=jnp.float32)
        local_top = jnp.max(logits, axis=1)
        local_total = jnp.sum(jnp.exp(logits - local_top[:, None]), axis=1)
        picked = jnp.sum(jnp.where(target_hits, logits, 0.0), axis=1)
        return (local_top, local_total, picked)

    policy_top, policy_total, policy_picked = local_stats(policy_all)
    refer_top, refer_total, refer_picked = local_stats(refer_all)
    top_policy, top_refer = lax.pmax((policy_top, refer_top), ("row", "col"))
    vocab_sums = lax.psum(
        (
            policy_total * jnp.exp(policy_top - top_policy),
            refer_total * jnp.exp(refer_top - top_refer),
            policy_picked,
            refer_picked,
        ),
        ("row", "col"),
    )
    policy_logprob = vocab_sums[2] - (top_policy + jnp.log(vocab_sums[0]))
    refer_logprob = vocab_sums[3] - (top_refer + jnp.log(vocab_sums[1]))
    difference = policy_logprob - refer_logprob
    one_hot = (segment[:, None] == jnp.arange(SEQS, dtype=jnp.int32)[None, :]).astype(jnp.float32)
    seq_sums = jnp.dot(difference, one_hot, precision=lax.Precision.HIGHEST)
    return seq_sums / seq_lengths.astype(jnp.float32)


def solution(mesh):
    placed = (
        P("row", "col"),
        P("col"),
        P("col", "row"),
        P("col", "row"),
        P("col", "row"),
        P("row", "col"),
        P("col"),
        P(None, "col", "row"),
        P(None, "col", "row"),
        P(None, "row", "col"),
        P("col"),
        P(None, ("row", "col")),
        P(),
        P(),
    )
    return jax.shard_map(per_device, mesh=mesh, in_specs=placed, out_specs=P(), check_vma=False)
```

profile of v0, /device:TPU:1, one launch (start us, length us, event | category | flops | bytes accessed | tf_op | source)
XLA Modules:
  0.0 926.4 jit_solution(10719453309221844499)
XLA Ops:
  6.5 0.9 fusion.48
  7.5 28.6 %psum.63 = f32[32]{0:T(128)S(1)} all-reduce(f32[32]{0:T(128)S(1)} %fusion.48), channel_id=1, replica_groups=mesh['row'=8,'col'=16] {'col'}, use_global_device_ids=true, to_apply=%region_1.0 | all-reduce | flops 32 | bytes 256 | tf_op jit(solution)/shard_map/psum | solution.py:47
  36.1 0.8 fusion.50
  36.9 28.5 %all_gather.24 = bf16[256,320]{1,0:T(8,128)(2,1)S(1)} all-gather(bf16[32,320]{1,0:T(8,128)(2,1)S(1)} %fusion.50), channel_id=1, replica_groups=mesh['row'=8,'col'=16] {'row'}, dimensions={0}, use_global_device_ids=true | all-gather | bytes 184320 | tf_op jit(solution)/shard_map/all_gather | solution.py:100
  65.4 2.5 fusion.21
  67.9 0.0 reduce-scatter.6.cloned.1.call-start
  67.9 0.2 reduce-window.8
  68.1 0.1 select_reduce_fusion
  68.2 0.1 fusion.30
  68.3 0.5 multiply_cosine_fusion
  68.9 126.3 %all-reduce.5.cloned.1.call-done = f32[256,896]{1,0:T(8,128)} async-done(((f32[256,896]{1,0:T(8,128)}), f32[256,896]{1,0:T(8,128)}) %all-reduce.5.cloned.1.call-update) | async-done | bytes 917520 | tf_op jit(solution)/shard_map/psum | solution.py:103
  195.2 1.1 slice.73
  196.3 0.2 copy.33
  196.6 0.2 copy.43
  196.9 0.2 copy.44
  197.1 0.9 slice_bitcast_fusion.4
  198.0 0.6 fusion.47
  198.6 0.2 subtract_convert_fusion
  198.8 0.5 fusion.62
  199.3 0.2 fusion.10
  199.4 1.3 convolution_convert_fusion
  200.7 1.1 fusion.65
  201.9 0.0 reduce-scatter.12.cloned.1.call-start
  202.0 4.0 slice_bitcast_fusion.2
  206.0 66.2 %reduce-scatter.6.cloned.1.call-done = f32[32,320]{1,0:T(8,128)} async-done(((f32[256,320]{1,0:T(8,128)}), f32[32,320]{1,0:T(8,128)}) %reduce-scatter.6.cloned.1.call-update) | async-done | bytes 40976 | tf_op jit(solution)/shard_map/reduce_scatter | solution.py:144
  272.1 0.8 fusion.51
  272.9 0.1 fusion.52
  273.0 29.0 %psum.65 = f32[32]{0:T(128)S(1)} all-reduce(f32[32]{0:T(128)S(1)} %fusion.52), channel_id=1, replica_groups=mesh['row'=8,'col'=16] {'col'}, use_global_device_ids=true, to_apply=%region_10.11 | all-reduce | flops 32 | bytes 256 | tf_op jit(solution)/shard_map/psum | solution.py:47
  302.1 0.1 fusion.54
  302.2 28.0 %all_gather.25 = bf16[256,320]{1,0:T(8,128)(2,1)S(1)} all-gather(bf16[32,320]{1,0:T(8,128)(2,1)S(1)} %fusion.54), channel_id=1, replica_groups=mesh['row'=8,'col'=16] {'row'}, dimensions={0}, use_global_device_ids=true | all-gather | bytes 184320 | tf_op jit(solution)/shard_map/all_gather | solution.py:153
  330.2 4.5 fusion.4
  334.7 0.0 reduce-scatter.8.cloned.1.call-start
  334.8 2.9 fusion
  337.7 0.0 reduce-scatter.14.cloned.1.call-start
  337.7 63.7 %reduce-scatter.12.cloned.1.call-done = f32[16,3456]{1,0:T(8,128)} async-done(((f32[256,3456]{1,0:T(8,128)}), f32[16,3456]{1,0:T(8,128)}) %reduce-scatter.12.cloned.1.call-update) | async-done | bytes 221200 | tf_op jit(solution)/shard_map/reduce_scatter | solution.py:54
  401.4 1.1 fusion.39
  402.5 24.7 %all_gather.29 = bf16[256,1728]{1,0:T(8,128)(2,1)S(1)} all-gather(bf16[16,1728]{1,0:T(8,128)(2,1)S(1)} %fusion.39), channel_id=1, replica_groups=mesh['row'=8,'col'=16] {'col'}, dimensions={0}, use_global_device_ids=true | all-gather | bytes 940032 | tf_op jit(solution)/shard_map/all_gather | solution.py:61
  427.2 1.4 fusion.11
  428.6 0.0 reduce-scatter.10.cloned.1.call-start
  428.7 42.0 %reduce-scatter.8.cloned.1.call-done = f32[16,3456]{1,0:T(8,128)} async-done(((f32[256,3456]{1,0:T(8,128)}), f32[16,3456]{1,0:T(8,128)}) %reduce-scatter.8.cloned.1.call-update) | async-done | bytes 221200 | tf_op jit(solution)/shard_map/reduce_scatter | solution.py:54
  470.6 1.1 fusion.40
  471.7 21.1 %all_gather.26 = bf16[256,1728]{1,0:T(8,128)(2,1)S(1)} all-gather(bf16[16,1728]{1,0:T(8,128)(2,1)S(1)} %fusion.40), channel_id=1, replica_groups=mesh['row'=8,'col'=16] {'col'}, dimensions={0}, use_global_device_ids=true | all-gather | bytes 940032 | tf_op jit(solution)/shard_map/all_gather | solution.py:61
  492.8 1.4 fusion.13
  494.2 0.0 all-gather.5.cloned.1.call-start
  494.2 50.7 %reduce-scatter.14.cloned.1.call-done = f32[32,320]{1,0:T(8,128)} async-done(((f32[256,320]{1,0:T(8,128)}), f32[32,320]{1,0:T(8,128)}) %reduce-scatter.14.cloned.1.call-update) | async-done | bytes 40976 | tf_op jit(solution)/shard_map/reduce_scatter | solution.py:63
  545.0 74.0 %reduce-scatter.10.cloned.1.call-done = f32[32,320]{1,0:T(8,128)} async-done(((f32[256,320]{1,0:T(8,128)}), f32[32,320]{1,0:T(8,128)}) %reduce-scatter.10.cloned.1.call-update) | async-done | bytes 40976 | tf_op jit(solution)/shard_map/reduce_scatter | solution.py:63
  618.9 0.9 multiply_reduce_fusion.1
  619.9 29.1 %all-reduce.2 = (f32[32]{0:T(128)S(1)}, f32[32]{0:T(128)S(1)}) all-reduce(f32[32]{0:T(128)S(1)} %get-tuple-element.30, f32[32]{0:T(128)S(1)} %get-tuple-element.28), channel_id=1, replica_groups=mesh['row'=8,'col'=16] {'col'}, use_global_device_ids=true, to_apply=%region_24.25 | all-reduce | flops 64 | bytes 512 | tf_op jit(solution)/shard_map/psum | solution.py:158
  649.0 0.9 fusion.55
  649.9 18.1 %all-gather = bf16[16,320,32]{1,2,0:T(8,128)(2,1)S(1)} all-gather(bf16[1,320,32]{1,2,0:T(8,128)(2,1)S(1)} %get-tuple-element.52), channel_id=1, replica_groups=mesh['row'=8,'col'=16] {'col'}, dimensions={0}, use_global_device_ids=true | all-gather | bytes 348160 | tf_op jit(solution)/shard_map/all_gather | solution.py:168
  667.9 0.1 copy.38
  668.1 1.0 reshape.255
  669.1 0.0 all-gather.7.cloned.1.call-start
  669.2 19.3 %all-gather.1 = bf16[16,320,32]{1,2,0:T(8,128)(2,1)S(1)} all-gather(bf16[1,320,32]{1,2,0:T(8,128)(2,1)S(1)} %get-tuple-element.53), channel_id=1, replica_groups=mesh['row'=8,'col'=16] {'col'}, dimensions={0}, use_global_device_ids=true | all-gather | bytes 348160 | tf_op jit(solution)/shard_map/all_gather | solution.py:169
  688.4 0.1 copy.39
  688.6 1.0 reshape.257
  689.6 35.1 %all-gather.5.cloned.1.call-done = bf16[256,5120]{1,0:T(8,128)(2,1)} async-done(((bf16[32,5120]{1,0:T(8,128)(2,1)}), bf16[256,5120]{1,0:T(8,128)(2,1)}) %all-gather.5.cloned.1.call-update) | async-done | bytes 2621456 | tf_op jit(solution)/shard_map/all_gather | solution.py:172
  724.8 5.9 fusion.63
  730.7 54.1 %all-gather.7.cloned.1.call-done = bf16[256,5120]{1,0:T(8,128)(2,1)} async-done(((bf16[32,5120]{1,0:T(8,128)(2,1)}), bf16[256,5120]{1,0:T(8,128)(2,1)}) %all-gather.7.cloned.1.call-update) | async-done | bytes 2621456 | tf_op jit(solution)/shard_map/all_gather | solution.py:173
  784.9 5.9 fusion.64
  790.8 65.0 %all-reduce.1 = (f32[256]{0:T(256)S(1)}, f32[256]{0:T(256)S(1)}) all-reduce(f32[256]{0:T(256)S(1)} %get-tuple-element.62, f32[256]{0:T(256)S(1)} %get-tuple-element.60), channel_id=1, replica_groups=mesh['row'=8,'col'=16] {'row','col'}, use_global_device_ids=true, to_apply=%region_28.29 | all-reduce | flops 512 | bytes 4096 | tf_op jit(solution)/shard_map/pmax | solution.py:189
  855.8 0.5 exponential_reduce_fusion.1
  856.3 62.5 %all-reduce = (f32[256]{0:T(256)S(1)}, f32[256]{0:T(256)S(1)}, f32[256]{0:T(256)S(1)}, f32[256]{0:T(256)S(1)}) all-reduce(f32[256]{0:T(256)S(1)} %get-tuple-element.54, f32[256]{0:T(256)S(1)} %exponential_multiply_fusion, f32[256]{0:T(256)S(1)} %get-tuple-element.18, ...), channel_id=1, replica_groups=mesh['row'=8,'col'=16] {'row','col'}, use_global_device_ids=true, to_apply=%region_26.27 | all-reduce | flops 1024 | bytes 8192 | tf_op jit(solution)/shard_map/psum | solution.py:190
  918.8 0.8 fusion.17
  (34 shorter events, 0.3 us)
Async XLA Ops:
  6.5 194.2 %copy-start = (bf16[640,320]{0,1:T(8,128)(2,1)S(1)}, bf16[640,320]{0,1:T(8,128)(2,1)}, u32[]{:S(2)}) copy-start(bf16[640,320]{0,1:T(8,128)(2,1)} %param.19) | copy-start | bytes 1228804
  6.5 61.4 %copy-start.5 = (s32[8]{0:T(128)S(1)}, s32[8]{0:T(128)}, u32[]{:S(2)}) copy-start(s32[8]{0:T(128)} %param.26) | copy-start | bytes 100
  6.5 188.7 %all-reduce.5.cloned.1.call-start = ((), (), s32[]{:S(2)}) async-start(), calls=%async_computation.5 | async-start | bytes 1835008 | tf_op jit(solution)/shard_map/psum | solution.py:103
  67.9 204.2 %reduce-scatter.6.cloned.1.call-start = ((), (), s32[]{:S(2)}) async-start(), calls=%async_computation.6 | async-start | bytes 442368 | tf_op jit(solution)/shard_map/reduce_scatter | solution.py:144
  201.9 70.2 %copy-start.1 = (bf16[32,320]{1,0:T(8,128)(2,1)S(1)}, bf16[32,320]{1,0:T(8,128)(2,1)}, u32[]{:S(2)}) copy-start(bf16[32,320]{1,0:T(8,128)(2,1)} %param.14) | copy-start | bytes 61444
  201.9 100.2 %copy-start.3 = (f32[320]{0:T(512)S(1)}, f32[320]{0:T(512)}, u32[]{:S(2)}) copy-start(f32[320]{0:T(512)} %param.20) | copy-start | bytes 3844
  201.9 199.5 %reduce-scatter.12.cloned.1.call-start = ((), (), s32[]{:S(2)}) async-start(), calls=%async_computation.10 | async-start | bytes 3760128 | tf_op jit(solution)/shard_map/reduce_scatter | solution.py:54
  334.7 135.9 %reduce-scatter.8.cloned.1.call-start = ((), (), s32[]{:S(2)}) async-start(), calls=%async_computation.7 | async-start | bytes 3760128 | tf_op jit(solution)/shard_map/reduce_scatter | solution.py:54
  337.6 89.5 %copy-start.6 = (bf16[2,1728,320]{1,2,0:T(8,128)(2,1)S(1)}, bf16[2,1728,320]{1,2,0:T(8,128)(2,1)}, u32[]{:S(2)}) copy-start(bf16[2,1728,320]{1,2,0:T(8,128)(2,1)} %param.23) | copy-start | bytes 6635524
  337.7 207.3 %reduce-scatter.14.cloned.1.call-start = ((), (), s32[]{:S(2)}) async-start(), calls=%async_computation.11 | async-start | bytes 442368 | tf_op jit(solution)/shard_map/reduce_scatter | solution.py:63
  428.6 220.3 %copy-start.2 = (f32[320]{0:T(512)S(1)}, f32[320]{0:T(512)}, u32[]{:S(2)}) copy-start(f32[320]{0:T(512)} %param.24) | copy-start | bytes 3844
  428.6 190.3 %reduce-scatter.10.cloned.1.call-start = ((), (), s32[]{:S(2)}) async-start(), calls=%async_computation.8 | async-start | bytes 442368 | tf_op jit(solution)/shard_map/reduce_scatter | solution.py:63
  494.2 230.6 %all-gather.5.cloned.1.call-start = ((), (), s32[]{:S(2)}) async-start(), calls=%async_computation.9 | async-start | bytes 2949120 | tf_op jit(solution)/shard_map/all_gather | solution.py:172
  669.1 115.8 %all-gather.7.cloned.1.call-start = ((), (), s32[]{:S(2)}) async-start(), calls=%async_computation.12 | async-start | bytes 2949120 | tf_op jit(solution)/shard_map/all_gather | solution.py:173
  730.7 125.1 %copy-start.4 = (s32[256]{0:T(256)S(1)}, s32[256]{0:T(256)}, u32[]{:S(2)}) copy-start(s32[256]{0:T(256)} %param.27) | copy-start | bytes 3076
Sparse Core Ops, SparseCore 0:
  68.0 127.1 all-reduce.4
  202.0 70.0 reduce-scatter.5
  334.9 66.4 reduce-scatter.11
  403.8 66.7 reduce-scatter.7
  474.5 70.4 reduce-scatter.13
  548.8 70.0 reduce-scatter.9
  669.2 55.4 all-gather.4
  727.3 57.4 all-gather.6
where the time goes:
time: 927 us; the launch traced here: 926 us
  waiting for transfers between devices  512 us (55%)
  blocking collectives  354 us (38%)
  matrix products  28.1 us (3%)
  between operations  13.7 us (1%)
    psum x1, waiting for transfers between devices, per_device(): joint_sums = lax.psum(joint_part, 'col')  126 us
    reduce_scatter x2, waiting for transfers between devices, feed_forward(): lax.psum_scatter(jnp.dot(row_block, down_weight, preferred_element_type=j...  125 us
    reduce_scatter x2, waiting for transfers between devices, feed_forward(): lax.psum_scatter(jnp.dot(row_block, gate_up, preferred_element_type=jnp.f...  106 us
    reduce_scatter x1, waiting for transfers between devices, per_device(): lax.psum_scatter(jnp.dot(attn_all, w_out, preferred_element_type=jnp.floa...  66.2 us
    pmax x1, blocking collectives, per_device(): top_policy, top_refer = lax.pmax((policy_top, refer_top), ('row', 'col'))  65 us
    psum x1, blocking collectives, per_device(): lax.psum((policy_total * jnp.exp(policy_top - top_policy), refer_total *...  62.5 us
    psum x2, blocking collectives, rms_local(): grand_total = lax.psum(squares, 'col')  57.7 us
    all_gather x1, waiting for transfers between devices, per_device(): lax.all_gather(wide_pair[1], 'row', axis=0, tiled=True)  54.1 us
  transfers between devices with their start and end apart: 8, of which 8 were waited for; matrix products, arithmetic and copies ran while one was open for 2% of the time, Pallas kernels for 0%

commit v1 on v0

v1 whole, which is shorter than its diff:
```python
import math

import jax
import jax.numpy as jnp
from jax import lax
from jax.experimental import pallas as pl
from jax.experimental.pallas import tpu as pltpu
from jax.sharding import PartitionSpec as P

T = 256
D = 5120
HEAD = 128
Q_HEADS = 5
QW = Q_HEADS * HEAD
QKV = QW + 2 * HEAD
SEQS = 8
FEAT = 320
CHIP = 2 * FEAT
FF = 1728
FFP = 1792
VOCAB = 640
ROWS = 8
COLS = 16
CHIPS = 8
EPSILON = 1e-06
ROPE_BASE = 1000000.0
MASKED = -1e30
MESH = pl.DeviceIdType.MESH
F32 = jnp.float32
BF16 = jnp.bfloat16


def remote(src, dst, send, recv, row, col):
    return pltpu.make_async_remote_copy(
        src_ref=src, dst_ref=dst, send_sem=send, recv_sem=recv,
        device_id={"row": row, "col": col}, device_id_type=MESH,
    )


def each(start, stop, body):
    def step(i, carry):
        body(i)
        return carry

    lax.fori_loop(start, stop, step, 0)


def split_sum(total, width):
    high = total.astype(BF16)
    low = (total - high.astype(F32)).astype(BF16)
    shape = (total.shape[0], width)
    return (
        jnp.broadcast_to(high.astype(F32), shape).astype(BF16),
        jnp.broadcast_to(low.astype(F32), shape).astype(BF16),
    )


def inverse_rms(total):
    return lax.rsqrt(total / D + EPSILON)


def layout_of(lens_ref, token):
    segment = jnp.zeros_like(token)
    start = jnp.zeros_like(token)
    end = jnp.int32(0)
    for s in range(SEQS):
        length = lens_ref[s]
        end = end + length
        before = end <= token
        segment = segment + jnp.where(before, 1, 0)
        start = start + jnp.where(before, length, 0)
    return segment, token - start


def kernel(
    res, attn_gain, w_query, w_key, w_value, w_out, mlp_gain, w_gate, w_up, w_down, final_gain, w_head, lens, targets,
    out,
    x_all, res_chip, wqkv, wo, wg, wu, wd, wh, mg, fg,
    part_send, part_recv, qkv_all, attended, proj_send, proj_recv, stream_all,
    gate_send, gate_recv, up_send, up_recv, hidden_all, down_send, down_recv,
    fin_a, fin_b, fin_c, logits, stat_send, stat_recv, stat2_recv,
    local_sem, swap_send, swap_recv, x_s, x_r, part_s, part_r, qkv_s, qkv_r, proj_s, proj_r, stream_s, stream_r,
    gu_s, gu_r, hid_s, hid_r, down_s, down_r, fin_s, fin_r, st_s, st_r, st2_s, st2_r,
):
    row, col = lax.axis_index("row"), lax.axis_index("col")
    core = lax.rem(col, 2)
    other = 1 - core
    chip = lax.div(col, 2)
    cx, zh = lax.div(row, 2), lax.rem(row, 2)
    cy, zl = lax.div(chip, 2), lax.rem(chip, 2)
    cz = zh * 2 + zl
    sib = chip * 2 + other

    def row_at(d):
        return lax.rem(row + d, ROWS)

    def chip_at(d):
        return lax.rem(chip + d, CHIPS)

    def col_at(d):
        return lax.rem(col + d, COLS)

    def at_xyz(x, y, z):
        return x * 2 + lax.div(z, 2), (y * 2 + lax.rem(z, 2)) * 2 + core

    mine = pl.ds(pl.multiple_of(core * FEAT, 64), FEAT)
    local = [
        (res, x_all.at[row]),
        (w_query, wqkv.at[:, 0:QW]),
        (w_key, wqkv.at[:, QW:QW + HEAD]),
        (w_value, wqkv.at[:, QW + HEAD:QKV]),
        (res, res_chip.at[core]),
        (mlp_gain, mg.at[core]),
        (final_gain, fg.at[core]),
        (w_out, wo.at[core]),
        (w_gate.at[core], wg.at[mine]),
        (w_up.at[core], wu.at[mine]),
        (w_down.at[core], wd.at[core]),
        (w_head, wh.at[core]),
    ]
    local = [pltpu.make_async_copy(s, d, local_sem.at[i]) for i, (s, d) in enumerate(local)]
    for copy in local:
        copy.start()

    barrier = pltpu.get_barrier_semaphore()

    def greet(r, c):
        pl.semaphore_signal(barrier, inc=1, device_id={"row": r, "col": c}, device_id_type=MESH)

    each(1, ROWS, lambda d: greet(row_at(d), col))
    each(1, ROWS, lambda d: greet(row_at(d), sib))
    each(1, COLS, lambda d: greet(row, col_at(d)))
    cross_z = lax.rem(cz + 1 + 2 * (1 - zl), 4)
    cross_row, cross_col = at_xyz(cx, cy, cross_z)
    greet(cross_row, cross_col)
    pl.semaphore_wait(barrier, 2 * (ROWS - 1) + (COLS - 1) + 1)

    def x_copy(d):
        return remote(res, x_all.at[row], x_s.at[d], x_r.at[d], row_at(d), col)

    each(1, ROWS, lambda d: x_copy(d).start())

    swaps = [
        (res, res_chip.at[core]),
        (mlp_gain, mg.at[core]),
        (final_gain, fg.at[core]),
        (w_out, wo.at[core]),
        (w_gate.at[other], wg.at[mine]),
        (w_up.at[other], wu.at[mine]),
        (w_down.at[other], wd.at[core]),
        (w_head, wh.at[core]),
    ]
    swaps = [remote(s, d, swap_send.at[i], swap_recv.at[i], row, sib) for i, (s, d) in enumerate(swaps)]
    for copy in swaps:
        copy.start()

    own_token = COLS * col + lax.broadcasted_iota(jnp.int32, (16, HEAD), 0)
    position = layout_of(lens, own_token)[1].astype(F32)
    lane = lax.broadcasted_iota(jnp.int32, (16, HEAD), 1)
    low_half = lane < HEAD // 2
    frequency = jnp.exp(jnp.where(low_half, lane, lane - HEAD // 2).astype(F32) * (-2.0 * math.log(ROPE_BASE) / HEAD))
    angle = position * frequency
    cosine = jnp.cos(angle)
    sine = jnp.where(low_half, -jnp.sin(angle), jnp.sin(angle))

    for i in range(4):
        local[i].wait()
    each(1, ROWS, lambda d: x_copy(d).wait_recv())

    x = x_all[...].reshape(T, FEAT).astype(F32)
    square_hi, square_lo = split_sum(jnp.sum(x * x, axis=1, keepdims=True), 64)
    xg = (x * attn_gain[...]).astype(BF16)
    part = jnp.dot(xg, wqkv[...], preferred_element_type=F32).astype(BF16)
    part_send[:, :, 0:QKV] = part.reshape(COLS, 16, QKV)
    part_send[:, :, QKV:QKV + 64] = square_hi.reshape(COLS, 16, 64)
    part_send[:, :, QKV + 64:QKV + 128] = square_lo.reshape(COLS, 16, 64)

    def part_copy(d):
        c = col_at(d)
        return remote(part_send.at[c], part_recv.at[d], part_s.at[d], part_r.at[d], row, c)

    each(1, COLS, lambda d: part_copy(d).start())
    part_recv[0] = part_send[col]
    each(1, COLS, lambda d: part_copy(d).wait_recv())

    total = jnp.sum(part_recv[...].astype(F32), axis=0)
    scale = inverse_rms(total[:, QKV:QKV + 1] + total[:, QKV + 64:QKV + 65])
    for h in range(Q_HEADS + 1):
        head = total[:, h * HEAD:(h + 1) * HEAD] * scale
        turned = head * cosine + pltpu.roll(head, HEAD // 2, 1) * sine
        qkv_all[chip, core, :, h * HEAD:(h + 1) * HEAD] = turned.astype(BF16)
    qkv_all[chip, core, :, QW + HEAD:QKV] = (total[:, QW + HEAD:QKV] * scale).astype(BF16)

    own_qkv = qkv_all.at[chip, core]
    own_kv = qkv_all.at[chip, core, :, QW:QKV]

    def qkv_copy(d):
        return remote(own_qkv, own_qkv, qkv_s.at[d], qkv_r.at[d], row, chip_at(d) * 2 + core)

    def kv_copy(d):
        return remote(own_kv, own_kv, qkv_s.at[CHIPS + d], qkv_r.at[CHIPS + d], row, chip_at(d) * 2 + other)

    each(1, CHIPS, lambda d: qkv_copy(d).start())
    each(0, CHIPS, lambda d: kv_copy(d).start())

    row_i = lax.broadcasted_iota(jnp.int32, (T // 2, 1), 0)
    q_token = lax.div(row_i, 16) * 32 + core * 16 + lax.rem(row_i, 16)
    k_token = lax.broadcasted_iota(jnp.int32, (1, T), 1)
    q_segment = layout_of(lens, q_token)[0]
    k_segment = layout_of(lens, k_token)[0]
    allowed = (q_segment == k_segment) & (k_token <= q_token)

    each(1, CHIPS, lambda d: qkv_copy(d).wait_recv())
    each(0, CHIPS, lambda d: kv_copy(d).wait_recv())

    keys = qkv_all[:, :, :, QW:QW + HEAD].reshape(T, HEAD)
    values = qkv_all[:, :, :, QW + HEAD:QKV].reshape(T, HEAD)
    for h in range(Q_HEADS):
        query = qkv_all[:, core, :, h * HEAD:(h + 1) * HEAD].reshape(T // 2, HEAD)
        scores = lax.dot_general(query, keys, (((1,), (1,)), ((), ())), preferred_element_type=F32)
        scores = jnp.where(allowed, scores * HEAD ** (-0.5), MASKED)
        weights = jnp.exp(scores - jnp.max(scores, axis=1, keepdims=True))
        weights = (weights / jnp.sum(weights, axis=1, keepdims=True)).astype(BF16)
        result = jnp.dot(weights, values, preferred_element_type=F32)
        attended[:, h * HEAD:(h + 1) * HEAD] = result.astype(BF16)

    for i in range(4, 8):
        local[i].wait()
    for i in range(0, 4):
        swaps[i].wait_recv()
    heads = attended[...]
    for j in range(2):
        half = jnp.dot(heads, wo[j], preferred_element_type=F32).astype(BF16)
        proj_send[:, :, j * FEAT:(j + 1) * FEAT] = half.reshape(ROWS, 16, FEAT)

    def proj_copy(d):
        r = row_at(d)
        return remote(proj_send.at[r], proj_recv.at[d], proj_s.at[d], proj_r.at[d], r, col)

    each(1, ROWS, lambda d: proj_copy(d).start())
    proj_recv[0] = proj_send[row]
    each(1, ROWS, lambda d: proj_copy(d).wait_recv())
    half_rows = pl.ds(pl.multiple_of(core * 16, 16), 16)
    residual = jnp.concatenate([res_chip[0, half_rows, :], res_chip[1, half_rows, :]], axis=1).astype(F32)
    stream_all[row, core] = (residual + jnp.sum(proj_recv[...].astype(F32), axis=0)).astype(BF16)

    own_stream = stream_all.at[row, core]

    def stream_copy(d):
        return remote(own_stream, own_stream, stream_s.at[d], stream_r.at[d], row_at(d), col)

    def stream_cross(d):
        return remote(own_stream, own_stream, stream_s.at[ROWS + d], stream_r.at[ROWS + d], row_at(d), sib)

    each(1, ROWS, lambda d: stream_copy(d).start())
    each(0, ROWS, lambda d: stream_cross(d).start())
    for i in range(8, 11):
        local[i].wait()
    for i in range(4, 6):
        swaps[i].wait_recv()
    each(1, ROWS, lambda d: stream_copy(d).wait_recv())
    each(0, ROWS, lambda d: stream_cross(d).wait_recv())

    stream = stream_all[...].reshape(T, CHIP).astype(F32)
    square_hi, square_lo = split_sum(jnp.sum(stream * stream, axis=1, keepdims=True), FFP - FF)
    gain = jnp.concatenate([mg[0], mg[1]], axis=1)
    xg = (stream * gain).astype(BF16)

    def gu_copy(kind, send, recv, d):
        c = chip_at(d)
        return remote(
            send.at[c], recv.at[d], gu_s.at[kind, d], gu_r.at[kind, d], row, c * 2 + core
        )

    gate_send[:, :, 0:FF] = jnp.dot(xg, wg[...], preferred_element_type=F32).astype(BF16).reshape(CHIPS, 32, FF)
    gate_send[:, :, FF:FFP] = square_hi.reshape(CHIPS, 32, FFP - FF)
    each(1, CHIPS, lambda d: gu_copy(0, gate_send, gate_recv, d).start())
    up_send[:, :, 0:FF] = jnp.dot(xg, wu[...], preferred_element_type=F32).astype(BF16).reshape(CHIPS, 32, FF)
    up_send[:, :, FF:FFP] = square_lo.reshape(CHIPS, 32, FFP - FF)
    each(1, CHIPS, lambda d: gu_copy(1, up_send, up_recv, d).start())
    gate_recv[0] = gate_send[chip]
    up_recv[0] = up_send[chip]
    each(1, CHIPS, lambda d: gu_copy(0, gate_send, gate_recv, d).wait_recv())
    each(1, CHIPS, lambda d: gu_copy(1, up_send, up_recv, d).wait_recv())
    gate_sum = jnp.sum(gate_recv[...].astype(F32), axis=0)
    up_sum = jnp.sum(up_recv[...].astype(F32), axis=0)
    scale = inverse_rms(gate_sum[:, FF:FF + 1] + up_sum[:, FF:FF + 1])
    gate = gate_sum[:, 0:FF] * scale
    hidden_all[chip] = (gate / (1.0 + jnp.exp(-gate)) * (up_sum[:, 0:FF] * scale)).astype(BF16)

    own_hidden = hidden_all.at[chip]

    def hid_copy(d):
        return remote(own_hidden, own_hidden, hid_s.at[d], hid_r.at[d], row, chip_at(d) * 2 + core)

    each(1, CHIPS, lambda d: hid_copy(d).start())
    swaps[6].wait_recv()
    each(1, CHIPS, lambda d: hid_copy(d).wait_recv())

    hidden = hidden_all[...].reshape(T, FF)
    for j in range(2):
        half = jnp.dot(hidden, wd[j], preferred_element_type=F32).astype(BF16)
        down_send[:, :, j * FEAT:(j + 1) * FEAT] = half.reshape(ROWS, 32, FEAT)

    def down_copy(d):
        r = row_at(d)
        return remote(down_send.at[r], down_recv.at[d], down_s.at[d], down_r.at[d], r, col)

    each(1, ROWS, lambda d: down_copy(d).start())
    down_recv[0] = down_send[row]
    each(1, ROWS, lambda d: down_copy(d).wait_recv())
    final = stream_all[row].reshape(32, CHIP).astype(F32) + jnp.sum(down_recv[...].astype(F32), axis=0)
    square_hi, square_lo = split_sum(jnp.sum(final * final, axis=1, keepdims=True), 64)
    final = (final * jnp.concatenate([fg[0], fg[1]], axis=1)).astype(BF16)

    fin_a[cy, zl, cx, zh] = final[:, 0:256]
    fin_b[cy, zl, cx, zh] = final[:, 256:512]
    fin_c[cy, zl, cx, zh, :, 0:128] = final[:, 512:640]
    fin_c[cy, zl, cx, zh, :, 128:192] = square_hi
    fin_c[cy, zl, cx, zh, :, 192:256] = square_lo

    parts = (fin_a, fin_b, fin_c)
    orders = ("zyx", "xzy", "yxz")

    def axis_copies(p, stage):
        order = orders[p]
        axis, done = order[stage], order[:stage]
        one = {"y": pl.ds(cy, 1), "x": pl.ds(cx, 1), "zl": pl.ds(zl, 1), "zh": pl.ds(zh, 1)}
        full = {"y": pl.ds(0, 4), "x": pl.ds(0, 4), "zl": pl.ds(0, 2), "zh": pl.ds(0, 2)}
        pick = {k: full[k] if k[0] in done else one[k] for k in one}
        ref = parts[p].at[pick["y"], pick["zl"], pick["x"], pick["zh"]]
        copies = []
        for d in (2, 1, 3):
            x = lax.rem(cx + d, 4) if axis == "x" else cx
            y = lax.rem(cy + d, 4) if axis == "y" else cy
            z = lax.rem(cz + d, 4) if axis == "z" else cz
            r, c = at_xyz(x, y, z)
            i = (p * 3 + stage) * 3 + d - 1
            copies.append(remote(ref, ref, fin_s.at[i], fin_r.at[i], r, c))
        return copies

    gathers = [[axis_copies(p, stage) for p in range(3)] for stage in range(3)]
    for stage in range(3):
        for p in range(3):
            if stage:
                for copy in gathers[stage - 1][p]:
                    copy.wait_recv()
            for copy in gathers[stage][p]:
                copy.start()
    local[11].wait()
    swaps[7].wait_recv()
    diagonal = lax.broadcasted_iota(jnp.int32, (T, T), 0) == lax.broadcasted_iota(jnp.int32, (T, T), 1)
    target = jnp.sum(jnp.where(diagonal, targets[...].astype(F32), 0.0), axis=1, keepdims=True).astype(jnp.int32)
    for p in range(3):
        for copy in gathers[2][p]:
            copy.wait_recv()

    square = jnp.zeros((T, 1), F32)
    for cc in range(CHIPS):
        a = fin_a[cc // 2, cc % 2].reshape(T, 256)
        b = fin_b[cc // 2, cc % 2].reshape(T, 256)
        c = fin_c[cc // 2, cc % 2].reshape(T, 256)
        square = square + c[:, 128:129].astype(F32) + c[:, 192:193].astype(F32)
        base = cc * CHIP
        for j in range(2):
            product = jnp.dot(a, wh[j, base:base + 256], preferred_element_type=F32)
            product += jnp.dot(b, wh[j, base + 256:base + 512], preferred_element_type=F32)
            product += jnp.dot(c[:, 0:128], wh[j, base + 512:base + 640], preferred_element_type=F32)
            if cc == 0:
                logits[j] = product
            else:
                logits[j] = logits[j] + product
    scale = inverse_rms(square)
    both = [logits[j] * scale for j in range(2)]
    top = jnp.maximum(*[jnp.max(l, axis=1, keepdims=True) for l in both])
    exponential = sum(jnp.sum(jnp.exp(l - top), axis=1, keepdims=True) for l in both)
    picked = jnp.zeros((T, 1), F32)
    for j in range(2):
        first = (row * COLS + chip * 2 + j) * VOCAB
        ids = first + lax.broadcasted_iota(jnp.int32, (T, VOCAB), 1)
        picked = picked + jnp.sum(jnp.where(ids == target, both[j], 0.0), axis=1, keepdims=True)
    lane = lax.broadcasted_iota(jnp.int32, (T, HEAD), 1)
    packed = jnp.where(lane == 0, top, jnp.where(lane == 1, exponential, picked))
    stat_recv[0] = jnp.transpose(packed)[0:8, :]

    def st_copy(d):
        return remote(stat_recv.at[0], stat_recv.at[d], st_s.at[d], st_r.at[d], row, chip_at(d) * 2 + core)

    each(1, CHIPS, lambda d: st_copy(d).start())
    each(1, CHIPS, lambda d: st_copy(d).wait_recv())

    def merge(blocks):
        top = jnp.max(blocks[:, 0:1, :], axis=0)
        exponential = jnp.sum(blocks[:, 1:2, :] * jnp.exp(blocks[:, 0:1, :] - top[None]), axis=0)
        return top, exponential, jnp.sum(blocks[:, 2:3, :], axis=0)

    top, exponential, picked = merge(stat_recv[...])
    line = lax.broadcasted_iota(jnp.int32, (8, T), 0)
    stat_send[...] = jnp.where(line == 0, top, jnp.where(line == 1, exponential, picked))
    own_stat = stat2_recv.at[core, row]
    stat2_recv[core, row] = stat_send[...]

    def st2_copy(d):
        return remote(stat_send, own_stat, st2_s.at[d], st2_r.at[d], row_at(d), col)

    def st2_cross(d):
        return remote(stat_send, own_stat, st2_s.at[ROWS + d], st2_r.at[ROWS + d], row_at(d), sib)

    each(1, ROWS, lambda d: st2_copy(d).start())
    each(0, ROWS, lambda d: st2_cross(d).start())
    each(1, ROWS, lambda d: st2_copy(d).wait_recv())
    each(0, ROWS, lambda d: st2_cross(d).wait_recv())
    logprob = []
    for m in range(2):
        top, exponential, picked = merge(stat2_recv[m])
        logprob.append(picked - (top + jnp.log(exponential)))
    difference = logprob[0] - logprob[1]
    hit = line == k_segment
    sums = jnp.sum(jnp.where(hit, difference, 0.0), axis=1, keepdims=True)
    length = jnp.sum(jnp.where(hit, 1.0, 0.0), axis=1, keepdims=True)
    square8 = lax.broadcasted_iota(jnp.int32, (8, 8), 0) == lax.broadcasted_iota(jnp.int32, (8, 8), 1)
    out[...] = jnp.sum(jnp.where(square8, sums / length, 0.0), axis=0, keepdims=True)

    each(1, ROWS, lambda d: x_copy(d).wait_send())
    for copy in swaps:
        copy.wait_send()
    each(1, COLS, lambda d: part_copy(d).wait_send())
    each(1, CHIPS, lambda d: qkv_copy(d).wait_send())
    each(0, CHIPS, lambda d: kv_copy(d).wait_send())
    each(1, ROWS, lambda d: proj_copy(d).wait_send())
    each(1, ROWS, lambda d: stream_copy(d).wait_send())
    each(0, ROWS, lambda d: stream_cross(d).wait_send())
    each(1, CHIPS, lambda d: gu_copy(0, gate_send, gate_recv, d).wait_send())
    each(1, CHIPS, lambda d: gu_copy(1, up_send, up_recv, d).wait_send())
    each(1, CHIPS, lambda d: hid_copy(d).wait_send())
    each(1, ROWS, lambda d: down_copy(d).wait_send())
    for stage in gathers:
        for copies in stage:
            for copy in copies:
                copy.wait_send()
    each(1, CHIPS, lambda d: st_copy(d).wait_send())
    each(1, ROWS, lambda d: st2_copy(d).wait_send())
    each(0, ROWS, lambda d: st2_cross(d).wait_send())


def per_device(
    residual, attn_gain, w_query, w_key, w_value, w_out, mlp_gain, w_gate, w_up, w_down, final_gain, w_head,
    seq_lengths, targets,
):
    anywhere = pl.BlockSpec(memory_space=pl.ANY)
    vmem = pl.BlockSpec(memory_space=pltpu.VMEM)
    smem = pl.BlockSpec(memory_space=pltpu.SMEM)
    dma = pltpu.SemaphoreType.DMA
    result = pl.pallas_call(
        kernel,
        out_shape=jax.ShapeDtypeStruct((1, SEQS), F32),
        in_specs=[anywhere, vmem] + [anywhere] * 10 + [smem, vmem],
        out_specs=vmem,
        scratch_shapes=[
            pltpu.VMEM((ROWS, 32, FEAT), BF16),
            pltpu.VMEM((2, 32, FEAT), BF16),
            pltpu.VMEM((FEAT, QKV), BF16),
            pltpu.VMEM((2, QW, FEAT), BF16),
            pltpu.VMEM((CHIP, FF), BF16),
            pltpu.VMEM((CHIP, FF), BF16),
            pltpu.VMEM((2, FF, FEAT), BF16),
            pltpu.VMEM((2, D, VOCAB), BF16),
            pltpu.VMEM((2, 1, FEAT), F32),
            pltpu.VMEM((2, 1, FEAT), F32),
            pltpu.VMEM((COLS, 16, QKV + 128), BF16),
            pltpu.VMEM((COLS, 16, QKV + 128), BF16),
            pltpu.VMEM((CHIPS, 2, 16, QKV), BF16),
            pltpu.VMEM((T // 2, QW), BF16),
            pltpu.VMEM((ROWS, 16, CHIP), BF16),
            pltpu.VMEM((ROWS, 16, CHIP), BF16),
            pltpu.VMEM((ROWS, 2, 16, CHIP), BF16),
            pltpu.VMEM((CHIPS, 32, FFP), BF16),
            pltpu.VMEM((CHIPS, 32, FFP), BF16),
            pltpu.VMEM((CHIPS, 32, FFP), BF16),
            pltpu.VMEM((CHIPS, 32, FFP), BF16),
            pltpu.VMEM((CHIPS, 32, FF), BF16),
            pltpu.VMEM((ROWS, 32, CHIP), BF16),
            pltpu.VMEM((ROWS, 32, CHIP), BF16),
            pltpu.VMEM((4, 2, 4, 2, 32, 256), BF16),
            pltpu.VMEM((4, 2, 4, 2, 32, 256), BF16),
            pltpu.VMEM((4, 2, 4, 2, 32, 256), BF16),
            pltpu.VMEM((2, T, VOCAB), F32),
            pltpu.VMEM((8, T), F32),
            pltpu.VMEM((CHIPS, 8, T), F32),
            pltpu.VMEM((2, ROWS, 8, T), F32),
            dma((12,)), dma((8,)), dma((8,)),
            dma((ROWS,)), dma((ROWS,)),
            dma((COLS,)), dma((COLS,)),
            dma((COLS,)), dma((COLS,)),
            dma((ROWS,)), dma((ROWS,)),
            dma((2 * ROWS,)), dma((2 * ROWS,)),
            dma((2, CHIPS)), dma((2, CHIPS)),
            dma((CHIPS,)), dma((CHIPS,)),
            dma((ROWS,)), dma((ROWS,)),
            dma((27,)), dma((27,)),
            dma((CHIPS,)), dma((CHIPS,)),
            dma((2 * ROWS,)), dma((2 * ROWS,)),
        ],
        compiler_params=pltpu.CompilerParams(
            collective_id=0, has_side_effects=True, vmem_limit_bytes=60 * 1024 * 1024
        ),
    )(
        residual, attn_gain.reshape(1, FEAT), w_query, w_key, w_value, w_out, mlp_gain.reshape(1, FEAT), w_gate, w_up,
        w_down, final_gain.reshape(1, FEAT), w_head, seq_lengths, targets.reshape(1, T),
    )
    return result.reshape(SEQS)


def solution(mesh):
    placed = (
        P("row", "col"), P("col"), P("col", "row"), P("col", "row"), P("col", "row"), P("row", "col"), P("col"),
        P(None, "col", "row"), P(None, "col", "row"), P(None, "row", "col"), P("col"), P(None, ("row", "col")), P(), P(),
    )
    return jax.shard_map(per_device, mesh=mesh, in_specs=placed, out_specs=P(), check_vma=False)
```

time: 927 us -> 145 us (0.16)
  waiting for transfers between devices: 512 us -> 0 us
  blocking collectives: 354 us -> 0 us
  Pallas kernels: 0 us -> 134 us
  matrix products: 28.1 us -> 0 us
  between operations: 13.7 us -> 0.01 us
    reduce_scatter x5 -> x0, waiting for transfers between devices: 296 us -> none  [the longest x2 125 us: feed_forward(): lax.psum_scatter(jnp.dot(row_block, down_weight, preferred_element_type=j...]
    psum x4 -> x0, blocking collectives: 149 us -> none  [the longest x1 62.5 us: per_device(): lax.psum((policy_total * jnp.exp(policy_top - top_policy), refer_total *...]
    all_gather x6 -> x0, blocking collectives: 140 us -> none  [the longest x2 45.8 us: feed_forward(): hidden_all = lax.all_gather(hidden, 'col', axis=0, tiled=True)]
    pallas_call x0 -> x1, Pallas kernels: none -> 134 us  [per_device(): pl.pallas_call(kernel, out_shape=jax.ShapeDtypeStruct((1, SEQS), F32), in...]
    psum x1 -> x0, waiting for transfers between devices: 126 us -> none  [per_device(): joint_sums = lax.psum(joint_part, 'col')]
    all_gather x2 -> x0, waiting for transfers between devices: 89.3 us -> none  [the longest x1 54.1 us: per_device(): lax.all_gather(wide_pair[1], 'row', axis=0, tiled=True)]
    pmax x1 -> x0, blocking collectives: 65 us -> none  [per_device(): top_policy, top_refer = lax.pmax((policy_top, refer_top), ('row', 'col'))]
    dot_general x11 -> x0, matrix products: 28.1 us -> none  [the longest x2 11.9 us: local_stats(): logits = jnp.dot(final_all, w_head, preferred_element_type=jnp.float32)]
  transfers between devices with their start and end apart: 8 -> 0, of which waited for: 8 -> 0; matrix products, arithmetic and copies ran while one was open for 2% -> 0% of each run, Pallas kernels for 0% -> 0%
where the time goes in v1:
time: 145 us
  Pallas kernels  134 us (92%)
  local copies, waits for them, and re-layouts  11.3 us (8%)
    pallas_call x1, Pallas kernels, per_device(): pl.pallas_call(kernel, out_shape=jax.ShapeDtypeStruct((1, SEQS), F32), in...  134 us
    unnamed x3, local copies, waits for them, and re-layouts  7.51 us

profile of v1, /device:TPU:1, one launch (start us, length us, event | category | flops | bytes accessed | tf_op | source)
XLA Modules:
  0.0 144.9 jit_solution(2472360048648890630)
XLA Ops:
  0.0 1.3 reshape.15.attn_gain
  1.3 1.2 reshape.16.mlp_gain
  2.5 1.3 reshape.17.final_gain
  3.8 2.0 %copy.15.w_out = bf16[640,320]{1,0:T(8,128)(2,1)} copy(bf16[640,320]{0,1:T(8,128)(2,1)} %param.19) | data formatting | bytes 819200 | tf_op args[5]
  5.8 4.4 %copy.16.w_down = bf16[2,1728,320]{2,1,0:T(8,128)(2,1)} copy(bf16[2,1728,320]{1,2,0:T(8,128)(2,1)} %param.23) | data formatting | bytes 4423680 | tf_op args[9]
  10.1 133.6 %shard_map.136 = f32[1,8]{1,0:T(1,128)} custom-call(bf16[32,320]{1,0:T(8,128)(2,1)} %res.1, f32[1,320]{1,0:T(1,128)} %reshape.15.attn_gain, bf16[320,640]{1,0:T(8,128)(2,1)} %w_query.1, bf16[320,128]{1,0:T(8,128)(2,1)} %w_key.1, bf16[320,128]{1,0:T(8,128)(2,1)} %w_value.1, bf16[640,320]{1,0:T(8,128)(2,1)} %copy.15.w_out, f32[1,320]{1,0:T(1,128)} %reshape.16.mlp_gain, ...), custom_call_target="tpu_custom_call" | custom-call | tf_op jit(solution)/shard_map/pallas_call | solution.py:454
  143.8 1.1 copy.18

commit v2 on v1

--- a/solution.py
+++ b/solution.py
@@ -45,6 +45,10 @@
     lax.fori_loop(start, stop, step, 0)
 
 
+def dot_nt(a, b):
+    return lax.dot_general(a, b, (((1,), (1,)), ((), ())), preferred_element_type=F32)
+
+
 def split_sum(total, width):
     high = total.astype(BF16)
     low = (total - high.astype(F32)).astype(BF16)
@@ -75,7 +79,7 @@
 def kernel(
     res, attn_gain, w_query, w_key, w_value, w_out, mlp_gain, w_gate, w_up, w_down, final_gain, w_head, lens, targets,
     out,
-    x_all, res_chip, wqkv, wo, wg, wu, wd, wh, mg, fg,
+    x_all, res_chip, wqkv, wo, wg, wu, wd, wh, gain_a, gain_m, gain_f, mg, fg,
     part_send, part_recv, qkv_all, attended, proj_send, proj_recv, stream_all,
     gate_send, gate_recv, up_send, up_recv, hidden_all, down_send, down_recv,
     fin_a, fin_b, fin_c, logits, stat_send, stat_recv, stat2_recv,
@@ -109,13 +113,14 @@
         (w_query, wqkv.at[:, 0:QW]),
         (w_key, wqkv.at[:, QW:QW + HEAD]),
         (w_value, wqkv.at[:, QW + HEAD:QKV]),
+        (attn_gain, gain_a),
+        (mlp_gain, gain_m),
+        (final_gain, gain_f),
         (res, res_chip.at[core]),
-        (mlp_gain, mg.at[core]),
-        (final_gain, fg.at[core]),
-        (w_out, wo.at[core]),
+        (w_out, wo.at[mine]),
         (w_gate.at[core], wg.at[mine]),
         (w_up.at[core], wu.at[mine]),
-        (w_down.at[core], wd.at[core]),
+        (w_down.at[core], wd.at[mine]),
         (w_head, wh.at[core]),
     ]
     local = [pltpu.make_async_copy(s, d, local_sem.at[i]) for i, (s, d) in enumerate(local)]
@@ -140,14 +145,18 @@
 
     each(1, ROWS, lambda d: x_copy(d).start())
 
+    for i in range(4, 7):
+        local[i].wait()
+    mg[core] = gain_m[...].reshape(1, FEAT)
+    fg[core] = gain_f[...].reshape(1, FEAT)
     swaps = [
         (res, res_chip.at[core]),
-        (mlp_gain, mg.at[core]),
-        (final_gain, fg.at[core]),
-        (w_out, wo.at[core]),
+        (mg.at[core], mg.at[core]),
+        (fg.at[core], fg.at[core]),
+        (w_out, wo.at[mine]),
         (w_gate.at[other], wg.at[mine]),
         (w_up.at[other], wu.at[mine]),
-        (w_down.at[other], wd.at[core]),
+        (w_down.at[other], wd.at[mine]),
         (w_head, wh.at[core]),
     ]
     swaps = [remote(s, d, swap_send.at[i], swap_recv.at[i], row, sib) for i, (s, d) in enumerate(swaps)]
@@ -169,7 +178,7 @@
 
     x = x_all[...].reshape(T, FEAT).astype(F32)
     square_hi, square_lo = split_sum(jnp.sum(x * x, axis=1, keepdims=True), 64)
-    xg = (x * attn_gain[...]).astype(BF16)
+    xg = (x * gain_a[...].reshape(1, FEAT)).astype(BF16)
     part = jnp.dot(xg, wqkv[...], preferred_element_type=F32).astype(BF16)
     part_send[:, :, 0:QKV] = part.reshape(COLS, 16, QKV)
     part_send[:, :, QKV:QKV + 64] = square_hi.reshape(COLS, 16, 64)
@@ -217,21 +226,18 @@
     values = qkv_all[:, :, :, QW + HEAD:QKV].reshape(T, HEAD)
     for h in range(Q_HEADS):
         query = qkv_all[:, core, :, h * HEAD:(h + 1) * HEAD].reshape(T // 2, HEAD)
-        scores = lax.dot_general(query, keys, (((1,), (1,)), ((), ())), preferred_element_type=F32)
+        scores = dot_nt(query, keys)
         scores = jnp.where(allowed, scores * HEAD ** (-0.5), MASKED)
         weights = jnp.exp(scores - jnp.max(scores, axis=1, keepdims=True))
         weights = (weights / jnp.sum(weights, axis=1, keepdims=True)).astype(BF16)
         result = jnp.dot(weights, values, preferred_element_type=F32)
         attended[:, h * HEAD:(h + 1) * HEAD] = result.astype(BF16)
 
-    for i in range(4, 8):
+    for i in range(7, 9):
         local[i].wait()
     for i in range(0, 4):
         swaps[i].wait_recv()
-    heads = attended[...]
-    for j in range(2):
-        half = jnp.dot(heads, wo[j], preferred_element_type=F32).astype(BF16)
-        proj_send[:, :, j * FEAT:(j + 1) * FEAT] = half.reshape(ROWS, 16, FEAT)
+    proj_send[...] = dot_nt(attended[...], wo[...]).astype(BF16).reshape(ROWS, 16, CHIP)
 
     def proj_copy(d):
         r = row_at(d)
@@ -254,7 +260,7 @@
 
     each(1, ROWS, lambda d: stream_copy(d).start())
     each(0, ROWS, lambda d: stream_cross(d).start())
-    for i in range(8, 11):
+    for i in range(9, 12):
         local[i].wait()
     for i in range(4, 6):
         swaps[i].wait_recv()
@@ -298,9 +304,7 @@
     each(1, CHIPS, lambda d: hid_copy(d).wait_recv())
 
     hidden = hidden_all[...].reshape(T, FF)
-    for j in range(2):
-        half = jnp.dot(hidden, wd[j], preferred_element_type=F32).astype(BF16)
-        down_send[:, :, j * FEAT:(j + 1) * FEAT] = half.reshape(ROWS, 32, FEAT)
+    down_send[...] = dot_nt(hidden, wd[...]).astype(BF16).reshape(ROWS, 32, CHIP)
 
     def down_copy(d):
         r = row_at(d)
@@ -347,7 +351,7 @@
                     copy.wait_recv()
             for copy in gathers[stage][p]:
                 copy.start()
-    local[11].wait()
+    local[12].wait()
     swaps[7].wait_recv()
     diagonal = lax.broadcasted_iota(jnp.int32, (T, T), 0) == lax.broadcasted_iota(jnp.int32, (T, T), 1)
     target = jnp.sum(jnp.where(diagonal, targets[...].astype(F32), 0.0), axis=1, keepdims=True).astype(jnp.int32)
@@ -454,17 +458,20 @@
     result = pl.pallas_call(
         kernel,
         out_shape=jax.ShapeDtypeStruct((1, SEQS), F32),
-        in_specs=[anywhere, vmem] + [anywhere] * 10 + [smem, vmem],
+        in_specs=[anywhere] * 12 + [smem, vmem],
         out_specs=vmem,
         scratch_shapes=[
             pltpu.VMEM((ROWS, 32, FEAT), BF16),
             pltpu.VMEM((2, 32, FEAT), BF16),
             pltpu.VMEM((FEAT, QKV), BF16),
-            pltpu.VMEM((2, QW, FEAT), BF16),
+            pltpu.VMEM((CHIP, QW), BF16),
             pltpu.VMEM((CHIP, FF), BF16),
             pltpu.VMEM((CHIP, FF), BF16),
-            pltpu.VMEM((2, FF, FEAT), BF16),
+            pltpu.VMEM((CHIP, FF), BF16),
             pltpu.VMEM((2, D, VOCAB), BF16),
+            pltpu.VMEM((FEAT,), F32),
+            pltpu.VMEM((FEAT,), F32),
+            pltpu.VMEM((FEAT,), F32),
             pltpu.VMEM((2, 1, FEAT), F32),
             pltpu.VMEM((2, 1, FEAT), F32),
             pltpu.VMEM((COLS, 16, QKV + 128), BF16),
@@ -488,7 +495,7 @@
             pltpu.VMEM((8, T), F32),
             pltpu.VMEM((CHIPS, 8, T), F32),
             pltpu.VMEM((2, ROWS, 8, T), F32),
-            dma((12,)), dma((8,)), dma((8,)),
+            dma((13,)), dma((8,)), dma((8,)),
             dma((ROWS,)), dma((ROWS,)),
             dma((COLS,)), dma((COLS,)),
             dma((COLS,)), dma((COLS,)),
@@ -505,8 +512,8 @@
             collective_id=0, has_side_effects=True, vmem_limit_bytes=60 * 1024 * 1024
         ),
     )(
-        residual, attn_gain.reshape(1, FEAT), w_query, w_key, w_value, w_out, mlp_gain.reshape(1, FEAT), w_gate, w_up,
-        w_down, final_gain.reshape(1, FEAT), w_head, seq_lengths, targets.reshape(1, T),
+        residual, attn_gain, w_query, w_key, w_value, w_out.T, mlp_gain, w_gate, w_up,
+        jnp.swapaxes(w_down, 1, 2), final_gain, w_head, seq_lengths, targets.reshape(1, T),
     )
     return result.reshape(SEQS)
 

time: 145 us -> 135 us (0.931)
  local copies, waits for them, and re-layouts: 11.3 us -> 1.19 us
    unnamed x3 -> x1, local copies, waits for them, and re-layouts: 7.51 us -> 1.19 us
    reshape x3 -> x0, local copies, waits for them, and re-layouts: 3.75 us -> none  [the longest x1 1.27 us: per_device(): final_gain.reshape(1, FEAT)]
where the time goes in v2:
time: 135 us
  Pallas kernels  134 us (99%)
    pallas_call x1, Pallas kernels, per_device(): pl.pallas_call(kernel, out_shape=jax.ShapeDtypeStruct((1, SEQS), F32), in...  134 us

profile of v2, /device:TPU:1, one launch (start us, length us, event | category | flops | bytes accessed | tf_op | source)
XLA Modules:
  0.0 135.0 jit_solution(5440848859692960807)
XLA Ops:
  0.0 133.8 %shard_map.136 = f32[1,8]{1,0:T(1,128)} custom-call(bf16[32,320]{1,0:T(8,128)(2,1)} %res.1, f32[320]{0:T(512)} %attn_gain.1, bf16[320,640]{1,0:T(8,128)(2,1)} %w_query.1, bf16[320,128]{1,0:T(8,128)(2,1)} %w_key.1, bf16[320,128]{1,0:T(8,128)(2,1)} %w_value.1, bf16[320,640]{1,0:T(8,128)(2,1)} %bitcast.5, f32[320]{0:T(512)} %mlp_gain.1, ...), custom_call_target="tpu_custom_call" | custom-call | tf_op jit(solution)/shard_map/pallas_call | solution.py:458
  133.8 1.2 copy.16

commit v3 on v2

--- a/solution.py
+++ b/solution.py
@@ -79,12 +79,12 @@
 def kernel(
     res, attn_gain, w_query, w_key, w_value, w_out, mlp_gain, w_gate, w_up, w_down, final_gain, w_head, lens, targets,
     out,
-    x_all, res_chip, wqkv, wo, wg, wu, wd, wh, gain_a, gain_m, gain_f, mg, fg,
-    part_send, part_recv, qkv_all, attended, proj_send, proj_recv, stream_all,
+    res_chip, square_all, x_all, wqkv, wo, wg, wu, wd, wh, gain_a, gain_m, gain_f, mg, fg,
+    part_own, part_pair, part_send, part_recv, qkv_all, attended, proj_send, proj_recv, stream_all,
     gate_send, gate_recv, up_send, up_recv, hidden_all, down_send, down_recv,
     fin_a, fin_b, fin_c, logits, stat_send, stat_recv, stat2_recv,
-    local_sem, swap_send, swap_recv, x_s, x_r, part_s, part_r, qkv_s, qkv_r, proj_s, proj_r, stream_s, stream_r,
-    gu_s, gu_r, hid_s, hid_r, down_s, down_r, fin_s, fin_r, st_s, st_r, st2_s, st2_r,
+    local_sem, swap_send, swap_recv, sq_s, sq_r, x_s, x_r, pair_s, pair_r, part_s, part_r, qkv_s, qkv_r, proj_s, proj_r,
+    stream_s, stream_r, gu_s, gu_r, hid_s, hid_r, down_s, down_r, fin_s, fin_r, st_s, st_r, st2_s, st2_r,
 ):
     row, col = lax.axis_index("row"), lax.axis_index("col")
     core = lax.rem(col, 2)
@@ -108,24 +108,46 @@
         return x * 2 + lax.div(z, 2), (y * 2 + lax.rem(z, 2)) * 2 + core
 
     mine = pl.ds(pl.multiple_of(core * FEAT, 64), FEAT)
-    local = [
-        (res, x_all.at[row]),
-        (w_query, wqkv.at[:, 0:QW]),
-        (w_key, wqkv.at[:, QW:QW + HEAD]),
-        (w_value, wqkv.at[:, QW + HEAD:QKV]),
-        (attn_gain, gain_a),
-        (mlp_gain, gain_m),
-        (final_gain, gain_f),
-        (res, res_chip.at[core]),
-        (w_out, wo.at[mine]),
-        (w_gate.at[core], wg.at[mine]),
-        (w_up.at[core], wu.at[mine]),
-        (w_down.at[core], wd.at[mine]),
-        (w_head, wh.at[core]),
-    ]
-    local = [pltpu.make_async_copy(s, d, local_sem.at[i]) for i, (s, d) in enumerate(local)]
-    for copy in local:
+    waits, pending, numbers = {}, [], {"own": 0, "pair": 0}
+
+    def own(name, src, dst):
+        copy = pltpu.make_async_copy(src, dst, local_sem.at[numbers["own"]])
+        numbers["own"] += 1
         copy.start()
+        waits.setdefault(name, []).append(copy.wait)
+
+    def swap(name, src, dst):
+        i = numbers["pair"]
+        numbers["pair"] += 1
+        copy = remote(src, dst, swap_send.at[i], swap_recv.at[i], row, sib)
+        copy.start()
+        waits.setdefault(name, []).append(copy.wait_recv)
+        pending.append(copy.wait_send)
+
+    def ready(*names):
+        for name in names:
+            for wait in waits.pop(name):
+                wait()
+
+    def start(first, stop, copy):
+        each(first, stop, lambda d: copy(d).start())
+        pending.append(lambda: each(first, stop, lambda d: copy(d).wait_send()))
+
+    def arrive(first, stop, copy):
+        each(first, stop, lambda d: copy(d).wait_recv())
+
+    def flush():
+        for finish in pending:
+            finish()
+        pending.clear()
+
+    own("residual", res, res_chip.at[core])
+    own("gains", attn_gain, gain_a)
+    own("gains", mlp_gain, gain_m)
+    own("gains", final_gain, gain_f)
+    own("wqkv", w_query, wqkv.at[:, 0:QW])
+    own("wqkv", w_key, wqkv.at[:, QW:QW + HEAD])
+    own("wqkv", w_value, wqkv.at[:, QW + HEAD:QKV])
 
     barrier = pltpu.get_barrier_semaphore()
 
@@ -140,28 +162,18 @@
     greet(cross_row, cross_col)
     pl.semaphore_wait(barrier, 2 * (ROWS - 1) + (COLS - 1) + 1)
 
-    def x_copy(d):
-        return remote(res, x_all.at[row], x_s.at[d], x_r.at[d], row_at(d), col)
-
-    each(1, ROWS, lambda d: x_copy(d).start())
-
-    for i in range(4, 7):
-        local[i].wait()
+    ready("residual", "gains")
+    x = res_chip[core].astype(F32)
+    eye = lax.broadcasted_iota(jnp.int32, (32, HEAD), 0) == lax.broadcasted_iota(jnp.int32, (32, HEAD), 1)
+    square = jnp.sum(jnp.where(eye, jnp.sum(x * x, axis=1, keepdims=True), 0.0), axis=0, keepdims=True)
+    square_all[0] = jnp.broadcast_to(square, (8, HEAD))
+
+    def sq_copy(d):
+        return remote(square_all.at[0], square_all.at[d], sq_s.at[d], sq_r.at[d], row, col_at(d))
+
+    start(1, COLS, sq_copy)
     mg[core] = gain_m[...].reshape(1, FEAT)
     fg[core] = gain_f[...].reshape(1, FEAT)
-    swaps = [
-        (res, res_chip.at[core]),
-        (mg.at[core], mg.at[core]),
-        (fg.at[core], fg.at[core]),
-        (w_out, wo.at[mine]),
-        (w_gate.at[other], wg.at[mine]),
-        (w_up.at[other], wu.at[mine]),
-        (w_down.at[other], wd.at[mine]),
-        (w_head, wh.at[core]),
-    ]
-    swaps = [remote(s, d, swap_send.at[i], swap_recv.at[i], row, sib) for i, (s, d) in enumerate(swaps)]
-    for copy in swaps:
-        copy.start()
 
     own_token = COLS * col + lax.broadcasted_iota(jnp.int32, (16, HEAD), 0)
     position = layout_of(lens, own_token)[1].astype(F32)
@@ -172,33 +184,49 @@
     cosine = jnp.cos(angle)
     sine = jnp.where(low_half, -jnp.sin(angle), jnp.sin(angle))
 
-    for i in range(4):
-        local[i].wait()
-    each(1, ROWS, lambda d: x_copy(d).wait_recv())
-
-    x = x_all[...].reshape(T, FEAT).astype(F32)
-    square_hi, square_lo = split_sum(jnp.sum(x * x, axis=1, keepdims=True), 64)
-    xg = (x * gain_a[...].reshape(1, FEAT)).astype(BF16)
-    part = jnp.dot(xg, wqkv[...], preferred_element_type=F32).astype(BF16)
-    part_send[:, :, 0:QKV] = part.reshape(COLS, 16, QKV)
-    part_send[:, :, QKV:QKV + 64] = square_hi.reshape(COLS, 16, 64)
-    part_send[:, :, QKV + 64:QKV + 128] = square_lo.reshape(COLS, 16, 64)
+    arrive(1, COLS, sq_copy)
+    square = jnp.sum(square_all[...], axis=0)[0:1]
+    square = jnp.sum(jnp.where(eye, square, 0.0), axis=1, keepdims=True)
+    x_all[row] = (x * inverse_rms(square) * gain_a[...].reshape(1, FEAT)).astype(BF16)
+
+    def x_copy(d):
+        return remote(x_all.at[row], x_all.at[row], x_s.at[d], x_r.at[d], row_at(d), col)
+
+    start(1, ROWS, x_copy)
+    swap("residual_pair", res_chip.at[core], res_chip.at[core])
+    swap("gains_pair", mg.at[core], mg.at[core])
+    swap("gains_pair", fg.at[core], fg.at[core])
+    own("wo", w_out, wo.at[mine])
+    swap("wo", w_out, wo.at[mine])
+    ready("wqkv")
+    arrive(1, ROWS, x_copy)
+
+    part = jnp.dot(x_all[...].reshape(T, FEAT), wqkv[...], preferred_element_type=F32)
+    part_own[...] = part.reshape(CHIPS, 2, 16, QKV)
+    pair = remote(part_own.at[:, other], part_pair, pair_s, pair_r, row, sib)
+    pair.start()
+    pending.append(pair.wait_send)
+    pair.wait_recv()
+    part_send[...] = part_own[:, core] + part_pair[...]
 
     def part_copy(d):
-        c = col_at(d)
-        return remote(part_send.at[c], part_recv.at[d], part_s.at[d], part_r.at[d], row, c)
-
-    each(1, COLS, lambda d: part_copy(d).start())
-    part_recv[0] = part_send[col]
-    each(1, COLS, lambda d: part_copy(d).wait_recv())
-
-    total = jnp.sum(part_recv[...].astype(F32), axis=0)
-    scale = inverse_rms(total[:, QKV:QKV + 1] + total[:, QKV + 64:QKV + 65])
+        c = chip_at(d)
+        return remote(part_send.at[c], part_recv.at[d], part_s.at[d], part_r.at[d], row, c * 2 + core)
+
+    start(1, CHIPS, part_copy)
+    own("wg", w_gate.at[core], wg.at[mine])
+    own("wu", w_up.at[core], wu.at[mine])
+    swap("wg", w_gate.at[other], wg.at[mine])
+    swap("wu", w_up.at[other], wu.at[mine])
+    part_recv[0] = part_send[chip]
+    arrive(1, CHIPS, part_copy)
+
+    total = jnp.sum(part_recv[...], axis=0)
     for h in range(Q_HEADS + 1):
-        head = total[:, h * HEAD:(h + 1) * HEAD] * scale
+        head = total[:, h * HEAD:(h + 1) * HEAD]
         turned = head * cosine + pltpu.roll(head, HEAD // 2, 1) * sine
         qkv_all[chip, core, :, h * HEAD:(h + 1) * HEAD] = turned.astype(BF16)
-    qkv_all[chip, core, :, QW + HEAD:QKV] = (total[:, QW + HEAD:QKV] * scale).astype(BF16)
+    qkv_all[chip, core, :, QW + HEAD:QKV] = total[:, QW + HEAD:QKV].astype(BF16)
 
     own_qkv = qkv_all.at[chip, core]
     own_kv = qkv_all.at[chip, core, :, QW:QKV]
@@ -209,8 +237,10 @@
     def kv_copy(d):
         return remote(own_kv, own_kv, qkv_s.at[CHIPS + d], qkv_r.at[CHIPS + d], row, chip_at(d) * 2 + other)
 
-    each(1, CHIPS, lambda d: qkv_copy(d).start())
-    each(0, CHIPS, lambda d: kv_copy(d).start())
+    start(1, CHIPS, qkv_copy)
+    start(0, CHIPS, kv_copy)
+    own("wd", w_down.at[core], wd.at[mine])
+    swap("wd", w_down.at[other], wd.at[mine])
 
     row_i = lax.broadcasted_iota(jnp.int32, (T // 2, 1), 0)
     q_token = lax.div(row_i, 16) * 32 + core * 16 + lax.rem(row_i, 16)
@@ -219,8 +249,8 @@
     k_segment = layout_of(lens, k_token)[0]
     allowed = (q_segment == k_segment) & (k_token <= q_token)
 
-    each(1, CHIPS, lambda d: qkv_copy(d).wait_recv())
-    each(0, CHIPS, lambda d: kv_copy(d).wait_recv())
+    arrive(1, CHIPS, qkv_copy)
+    arrive(0, CHIPS, kv_copy)
 
     keys = qkv_all[:, :, :, QW:QW + HEAD].reshape(T, HEAD)
     values = qkv_all[:, :, :, QW + HEAD:QKV].reshape(T, HEAD)
@@ -233,22 +263,19 @@
         result = jnp.dot(weights, values, preferred_element_type=F32)
         attended[:, h * HEAD:(h + 1) * HEAD] = result.astype(BF16)
 
-    for i in range(7, 9):
-        local[i].wait()
-    for i in range(0, 4):
-        swaps[i].wait_recv()
-    proj_send[...] = dot_nt(attended[...], wo[...]).astype(BF16).reshape(ROWS, 16, CHIP)
+    ready("wo", "residual_pair")
+    proj_send[...] = dot_nt(attended[...], wo[...]).reshape(ROWS, 16, CHIP)
 
     def proj_copy(d):
         r = row_at(d)
         return remote(proj_send.at[r], proj_recv.at[d], proj_s.at[d], proj_r.at[d], r, col)
 
-    each(1, ROWS, lambda d: proj_copy(d).start())
+    start(1, ROWS, proj_copy)
     proj_recv[0] = proj_send[row]
-    each(1, ROWS, lambda d: proj_copy(d).wait_recv())
+    arrive(1, ROWS, proj_copy)
     half_rows = pl.ds(pl.multiple_of(core * 16, 16), 16)
     residual = jnp.concatenate([res_chip[0, half_rows, :], res_chip[1, half_rows, :]], axis=1).astype(F32)
-    stream_all[row, core] = (residual + jnp.sum(proj_recv[...].astype(F32), axis=0)).astype(BF16)
+    stream_all[row, core] = (residual + jnp.sum(proj_recv[...], axis=0)).astype(BF16)
 
     own_stream = stream_all.at[row, core]
 
@@ -258,14 +285,14 @@
     def stream_cross(d):
         return remote(own_stream, own_stream, stream_s.at[ROWS + d], stream_r.at[ROWS + d], row_at(d), sib)
 
-    each(1, ROWS, lambda d: stream_copy(d).start())
-    each(0, ROWS, lambda d: stream_cross(d).start())
-    for i in range(9, 12):
-        local[i].wait()
-    for i in range(4, 6):
-        swaps[i].wait_recv()
-    each(1, ROWS, lambda d: stream_copy(d).wait_recv())
-    each(0, ROWS, lambda d: stream_cross(d).wait_recv())
+    start(1, ROWS, stream_copy)
+    start(0, ROWS, stream_cross)
+    own("wh", w_head, wh.at[core])
+    swap("wh", w_head, wh.at[core])
+    wh_at = len(pending) - 1
+    ready("wg", "wu", "gains_pair")
+    arrive(1, ROWS, stream_copy)
+    arrive(0, ROWS, stream_cross)
 
     stream = stream_all[...].reshape(T, CHIP).astype(F32)
     square_hi, square_lo = split_sum(jnp.sum(stream * stream, axis=1, keepdims=True), FFP - FF)
@@ -280,15 +307,20 @@
 
     gate_send[:, :, 0:FF] = jnp.dot(xg, wg[...], preferred_element_type=F32).astype(BF16).reshape(CHIPS, 32, FF)
     gate_send[:, :, FF:FFP] = square_hi.reshape(CHIPS, 32, FFP - FF)
-    each(1, CHIPS, lambda d: gu_copy(0, gate_send, gate_recv, d).start())
+    start(1, CHIPS, lambda d: gu_copy(0, gate_send, gate_recv, d))
     up_send[:, :, 0:FF] = jnp.dot(xg, wu[...], preferred_element_type=F32).astype(BF16).reshape(CHIPS, 32, FF)
     up_send[:, :, FF:FFP] = square_lo.reshape(CHIPS, 32, FFP - FF)
-    each(1, CHIPS, lambda d: gu_copy(1, up_send, up_recv, d).start())
+    start(1, CHIPS, lambda d: gu_copy(1, up_send, up_recv, d))
     gate_recv[0] = gate_send[chip]
     up_recv[0] = up_send[chip]
-    each(1, CHIPS, lambda d: gu_copy(0, gate_send, gate_recv, d).wait_recv())
-    each(1, CHIPS, lambda d: gu_copy(1, up_send, up_recv, d).wait_recv())
+    held = pending[-2:]
+    del pending[-2:]
+    wh_swap = [pending.pop(i) for i in (wh_at,)]
+    flush()
+    pending.extend(wh_swap + held)
+    arrive(1, CHIPS, lambda d: gu_copy(0, gate_send, gate_recv, d))
     gate_sum = jnp.sum(gate_recv[...].astype(F32), axis=0)
+    arrive(1, CHIPS, lambda d: gu_copy(1, up_send, up_recv, d))
     up_sum = jnp.sum(up_recv[...].astype(F32), axis=0)
     scale = inverse_rms(gate_sum[:, FF:FF + 1] + up_sum[:, FF:FF + 1])
     gate = gate_sum[:, 0:FF] * scale
@@ -299,21 +331,21 @@
     def hid_copy(d):
         return remote(own_hidden, own_hidden, hid_s.at[d], hid_r.at[d], row, chip_at(d) * 2 + core)
 
-    each(1, CHIPS, lambda d: hid_copy(d).start())
-    swaps[6].wait_recv()
-    each(1, CHIPS, lambda d: hid_copy(d).wait_recv())
+    start(1, CHIPS, hid_copy)
+    ready("wd")
+    arrive(1, CHIPS, hid_copy)
 
     hidden = hidden_all[...].reshape(T, FF)
-    down_send[...] = dot_nt(hidden, wd[...]).astype(BF16).reshape(ROWS, 32, CHIP)
+    down_send[...] = dot_nt(hidden, wd[...]).reshape(ROWS, 32, CHIP)
 
     def down_copy(d):
         r = row_at(d)
         return remote(down_send.at[r], down_recv.at[d], down_s.at[d], down_r.at[d], r, col)
 
-    each(1, ROWS, lambda d: down_copy(d).start())
+    start(1, ROWS, down_copy)
     down_recv[0] = down_send[row]
-    each(1, ROWS, lambda d: down_copy(d).wait_recv())
-    final = stream_all[row].reshape(32, CHIP).astype(F32) + jnp.sum(down_recv[...].astype(F32), axis=0)
+    arrive(1, ROWS, down_copy)
+    final = stream_all[row].reshape(32, CHIP).astype(F32) + jnp.sum(down_recv[...], axis=0)
     square_hi, square_lo = split_sum(jnp.sum(final * final, axis=1, keepdims=True), 64)
     final = (final * jnp.concatenate([fg[0], fg[1]], axis=1)).astype(BF16)
 
@@ -351,8 +383,12 @@
                     copy.wait_recv()
             for copy in gathers[stage][p]:
                 copy.start()
-    local[12].wait()
-    swaps[7].wait_recv()
+                pending.append(copy.wait_send)
+    last = pending[-9:]
+    del pending[-9:]
+    flush()
+    pending.extend(last)
+    ready("wh")
     diagonal = lax.broadcasted_iota(jnp.int32, (T, T), 0) == lax.broadcasted_iota(jnp.int32, (T, T), 1)
     target = jnp.sum(jnp.where(diagonal, targets[...].astype(F32), 0.0), axis=1, keepdims=True).astype(jnp.int32)
     for p in range(3):
@@ -360,20 +396,16 @@
             copy.wait_recv()
 
     square = jnp.zeros((T, 1), F32)
-    for cc in range(CHIPS):
-        a = fin_a[cc // 2, cc % 2].reshape(T, 256)
-        b = fin_b[cc // 2, cc % 2].reshape(T, 256)
-        c = fin_c[cc // 2, cc % 2].reshape(T, 256)
-        square = square + c[:, 128:129].astype(F32) + c[:, 192:193].astype(F32)
-        base = cc * CHIP
+    for y in range(4):
+        pieces = []
+        for z in range(2):
+            c = fin_c[y, z].reshape(T, 256)
+            square = square + c[:, 128:129].astype(F32) + c[:, 192:193].astype(F32)
+            pieces += [fin_a[y, z].reshape(T, 256), fin_b[y, z].reshape(T, 256), c[:, 0:128]]
+        states = jnp.concatenate(pieces, axis=1)
         for j in range(2):
-            product = jnp.dot(a, wh[j, base:base + 256], preferred_element_type=F32)
-            product += jnp.dot(b, wh[j, base + 256:base + 512], preferred_element_type=F32)
-            product += jnp.dot(c[:, 0:128], wh[j, base + 512:base + 640], preferred_element_type=F32)
-            if cc == 0:
-                logits[j] = product
-            else:
-                logits[j] = logits[j] + product
+            product = jnp.dot(states, wh[j, y * 2 * CHIP:(y + 1) * 2 * CHIP], preferred_element_type=F32)
+            logits[j] = product if y == 0 else logits[j] + product
     scale = inverse_rms(square)
     both = [logits[j] * scale for j in range(2)]
     top = jnp.maximum(*[jnp.max(l, axis=1, keepdims=True) for l in both])
@@ -390,8 +422,8 @@
     def st_copy(d):
         return remote(stat_recv.at[0], stat_recv.at[d], st_s.at[d], st_r.at[d], row, chip_at(d) * 2 + core)
 
-    each(1, CHIPS, lambda d: st_copy(d).start())
-    each(1, CHIPS, lambda d: st_copy(d).wait_recv())
+    start(1, CHIPS, st_copy)
+    arrive(1, CHIPS, st_copy)
 
     def merge(blocks):
         top = jnp.max(blocks[:, 0:1, :], axis=0)
@@ -410,10 +442,10 @@
     def st2_cross(d):
         return remote(stat_send, own_stat, st2_s.at[ROWS + d], st2_r.at[ROWS + d], row_at(d), sib)
 
-    each(1, ROWS, lambda d: st2_copy(d).start())
-    each(0, ROWS, lambda d: st2_cross(d).start())
-    each(1, ROWS, lambda d: st2_copy(d).wait_recv())
-    each(0, ROWS, lambda d: st2_cross(d).wait_recv())
+    start(1, ROWS, st2_copy)
+    start(0, ROWS, st2_cross)
+    arrive(1, ROWS, st2_copy)
+    arrive(0, ROWS, st2_cross)
     logprob = []
     for m in range(2):
         top, exponential, picked = merge(stat2_recv[m])
@@ -425,26 +457,7 @@
     square8 = lax.broadcasted_iota(jnp.int32, (8, 8), 0) == lax.broadcasted_iota(jnp.int32, (8, 8), 1)
     out[...] = jnp.sum(jnp.where(square8, sums / length, 0.0), axis=0, keepdims=True)
 
-    each(1, ROWS, lambda d: x_copy(d).wait_send())
-    for copy in swaps:
-        copy.wait_send()
-    each(1, COLS, lambda d: part_copy(d).wait_send())
-    each(1, CHIPS, lambda d: qkv_copy(d).wait_send())
-    each(0, CHIPS, lambda d: kv_copy(d).wait_send())
-    each(1, ROWS, lambda d: proj_copy(d).wait_send())
-    each(1, ROWS, lambda d: stream_copy(d).wait_send())
-    each(0, ROWS, lambda d: stream_cross(d).wait_send())
-    each(1, CHIPS, lambda d: gu_copy(0, gate_send, gate_recv, d).wait_send())
-    each(1, CHIPS, lambda d: gu_copy(1, up_send, up_recv, d).wait_send())
-    each(1, CHIPS, lambda d: hid_copy(d).wait_send())
-    each(1, ROWS, lambda d: down_copy(d).wait_send())
-    for stage in gathers:
-        for copies in stage:
-            for copy in copies:
-                copy.wait_send()
-    each(1, CHIPS, lambda d: st_copy(d).wait_send())
-    each(1, ROWS, lambda d: st2_copy(d).wait_send())
-    each(0, ROWS, lambda d: st2_cross(d).wait_send())
+    flush()
 
 
 def per_device(
@@ -461,8 +474,9 @@
         in_specs=[anywhere] * 12 + [smem, vmem],
         out_specs=vmem,
         scratch_shapes=[
+            pltpu.VMEM((2, 32, FEAT), BF16),
+            pltpu.VMEM((COLS, 8, HEAD), F32),
             pltpu.VMEM((ROWS, 32, FEAT), BF16),
-            pltpu.VMEM((2, 32, FEAT), BF16),
             pltpu.VMEM((FEAT, QKV), BF16),
             pltpu.VMEM((CHIP, QW), BF16),
             pltpu.VMEM((CHIP, FF), BF16),
@@ -474,20 +488,22 @@
             pltpu.VMEM((FEAT,), F32),
             pltpu.VMEM((2, 1, FEAT), F32),
             pltpu.VMEM((2, 1, FEAT), F32),
-            pltpu.VMEM((COLS, 16, QKV + 128), BF16),
-            pltpu.VMEM((COLS, 16, QKV + 128), BF16),
+            pltpu.VMEM((CHIPS, 2, 16, QKV), F32),
+            pltpu.VMEM((CHIPS, 16, QKV), F32),
+            pltpu.VMEM((CHIPS, 16, QKV), F32),
+            pltpu.VMEM((CHIPS, 16, QKV), F32),
             pltpu.VMEM((CHIPS, 2, 16, QKV), BF16),
             pltpu.VMEM((T // 2, QW), BF16),
-            pltpu.VMEM((ROWS, 16, CHIP), BF16),
-            pltpu.VMEM((ROWS, 16, CHIP), BF16),
+            pltpu.VMEM((ROWS, 16, CHIP), F32),
+            pltpu.VMEM((ROWS, 16, CHIP), F32),
             pltpu.VMEM((ROWS, 2, 16, CHIP), BF16),
             pltpu.VMEM((CHIPS, 32, FFP), BF16),
             pltpu.VMEM((CHIPS, 32, FFP), BF16),
             pltpu.VMEM((CHIPS, 32, FFP), BF16),
             pltpu.VMEM((CHIPS, 32, FFP), BF16),
             pltpu.VMEM((CHIPS, 32, FF), BF16),
-            pltpu.VMEM((ROWS, 32, CHIP), BF16),
-            pltpu.VMEM((ROWS, 32, CHIP), BF16),
+            pltpu.VMEM((ROWS, 32, CHIP), F32),
+            pltpu.VMEM((ROWS, 32, CHIP), F32),
             pltpu.VMEM((4, 2, 4, 2, 32, 256), BF16),
             pltpu.VMEM((4, 2, 4, 2, 32, 256), BF16),
             pltpu.VMEM((4, 2, 4, 2, 32, 256), BF16),
@@ -495,9 +511,11 @@
             pltpu.VMEM((8, T), F32),
             pltpu.VMEM((CHIPS, 8, T), F32),
             pltpu.VMEM((2, ROWS, 8, T), F32),
-            dma((13,)), dma((8,)), dma((8,)),
+            dma((12,)), dma((8,)), dma((8,)),
+            dma((COLS,)), dma((COLS,)),
             dma((ROWS,)), dma((ROWS,)),
-            dma((COLS,)), dma((COLS,)),
+            dma, dma,
+            dma((CHIPS,)), dma((CHIPS,)),
             dma((COLS,)), dma((COLS,)),
             dma((ROWS,)), dma((ROWS,)),
             dma((2 * ROWS,)), dma((2 * ROWS,)),

time: 135 us -> 143 us (1.059)
  Pallas kernels: 134 us -> 142 us
    pallas_call x1, Pallas kernels: 134 us -> 142 us  [per_device(): pl.pallas_call(kernel, out_shape=jax.ShapeDtypeStruct((1, SEQS), F32), in...]
where the time goes in v3:
time: 143 us
  Pallas kernels  142 us (99%)
    pallas_call x1, Pallas kernels, per_device(): pl.pallas_call(kernel, out_shape=jax.ShapeDtypeStruct((1, SEQS), F32), in...  142 us

profile of v3, /device:TPU:1, one launch (start us, length us, event | category | flops | bytes accessed | tf_op | source)
XLA Modules:
  0.0 143.2 jit_solution(16239641237868079356)
XLA Ops:
  0.0 142.0 %shard_map.136 = f32[1,8]{1,0:T(1,128)} custom-call(bf16[32,320]{1,0:T(8,128)(2,1)} %res.1, f32[320]{0:T(512)} %attn_gain.1, bf16[320,640]{1,0:T(8,128)(2,1)} %w_query.1, bf16[320,128]{1,0:T(8,128)(2,1)} %w_key.1, bf16[320,128]{1,0:T(8,128)(2,1)} %w_value.1, bf16[320,640]{1,0:T(8,128)(2,1)} %bitcast.5, f32[320]{0:T(512)} %mlp_gain.1, ...), custom_call_target="tpu_custom_call" | custom-call | tf_op jit(solution)/shard_map/pallas_call | solution.py:471
  142.0 1.2 copy.16

commit v4 on v3

--- a/solution.py
+++ b/solution.py
@@ -18,6 +18,8 @@
 CHIP = 2 * FEAT
 FF = 1728
 FFP = 1792
+HALF = FFP // 2
+CHUNKS = ((HALF, FF - HALF), (0, HALF))
 VOCAB = 640
 ROWS = 8
 COLS = 16
@@ -79,9 +81,9 @@
 def kernel(
     res, attn_gain, w_query, w_key, w_value, w_out, mlp_gain, w_gate, w_up, w_down, final_gain, w_head, lens, targets,
     out,
-    res_chip, square_all, x_all, wqkv, wo, wg, wu, wd, wh, gain_a, gain_m, gain_f, mg, fg,
+    target_row, res_chip, square_all, x_all, wqkv, wo, wg, wu, wd, wh, gain_a, gain_m, gain_f, mg, fg,
     part_own, part_pair, part_send, part_recv, qkv_all, attended, proj_send, proj_recv, stream_all,
-    gate_send, gate_recv, up_send, up_recv, hidden_all, down_send, down_recv,
+    gu_send, gu_recv, hidden_all, down_send, down_recv,
     fin_a, fin_b, fin_c, logits, stat_send, stat_recv, stat2_recv,
     local_sem, swap_send, swap_recv, sq_s, sq_r, x_s, x_r, pair_s, pair_r, part_s, part_r, qkv_s, qkv_r, proj_s, proj_r,
     stream_s, stream_r, gu_s, gu_r, hid_s, hid_r, down_s, down_r, fin_s, fin_r, st_s, st_r, st2_s, st2_r,
@@ -142,6 +144,7 @@
         pending.clear()
 
     own("residual", res, res_chip.at[core])
+    own("targets", targets, target_row)
     own("gains", attn_gain, gain_a)
     own("gains", mlp_gain, gain_m)
     own("gains", final_gain, gain_f)
@@ -295,48 +298,58 @@
     arrive(0, ROWS, stream_cross)
 
     stream = stream_all[...].reshape(T, CHIP).astype(F32)
-    square_hi, square_lo = split_sum(jnp.sum(stream * stream, axis=1, keepdims=True), FFP - FF)
+    square_hi, square_lo = split_sum(jnp.sum(stream * stream, axis=1, keepdims=True), HALF - CHUNKS[0][1])
     gain = jnp.concatenate([mg[0], mg[1]], axis=1)
     xg = (stream * gain).astype(BF16)
 
-    def gu_copy(kind, send, recv, d):
-        c = chip_at(d)
-        return remote(
-            send.at[c], recv.at[d], gu_s.at[kind, d], gu_r.at[kind, d], row, c * 2 + core
-        )
-
-    gate_send[:, :, 0:FF] = jnp.dot(xg, wg[...], preferred_element_type=F32).astype(BF16).reshape(CHIPS, 32, FF)
-    gate_send[:, :, FF:FFP] = square_hi.reshape(CHIPS, 32, FFP - FF)
-    start(1, CHIPS, lambda d: gu_copy(0, gate_send, gate_recv, d))
-    up_send[:, :, 0:FF] = jnp.dot(xg, wu[...], preferred_element_type=F32).astype(BF16).reshape(CHIPS, 32, FF)
-    up_send[:, :, FF:FFP] = square_lo.reshape(CHIPS, 32, FFP - FF)
-    start(1, CHIPS, lambda d: gu_copy(1, up_send, up_recv, d))
-    gate_recv[0] = gate_send[chip]
-    up_recv[0] = up_send[chip]
+    def gu_copy(i):
+        def copy(d):
+            c = chip_at(d)
+            return remote(gu_send.at[i, c], gu_recv.at[i, d], gu_s.at[i, d], gu_r.at[i, d], row, c * 2 + core)
+
+        return copy
+
+    for i, (low, width) in enumerate(CHUNKS):
+        for half, weight in enumerate((wg, wu)):
+            product = jnp.dot(xg, weight[:, low:low + width], preferred_element_type=F32)
+            gu_send[i, :, :, half * HALF:half * HALF + width] = product.astype(BF16).reshape(CHIPS, 32, width)
+        if i == 0:
+            gu_send[0, :, :, width:HALF] = square_hi.reshape(CHIPS, 32, HALF - width)
+            gu_send[0, :, :, HALF + width:FFP] = square_lo.reshape(CHIPS, 32, HALF - width)
+        start(1, CHIPS, gu_copy(i))
+        gu_recv[i, 0] = gu_send[i, chip]
     held = pending[-2:]
     del pending[-2:]
-    wh_swap = [pending.pop(i) for i in (wh_at,)]
+    wh_swap = pending.pop(wh_at)
     flush()
-    pending.extend(wh_swap + held)
-    arrive(1, CHIPS, lambda d: gu_copy(0, gate_send, gate_recv, d))
-    gate_sum = jnp.sum(gate_recv[...].astype(F32), axis=0)
-    arrive(1, CHIPS, lambda d: gu_copy(1, up_send, up_recv, d))
-    up_sum = jnp.sum(up_recv[...].astype(F32), axis=0)
-    scale = inverse_rms(gate_sum[:, FF:FF + 1] + up_sum[:, FF:FF + 1])
-    gate = gate_sum[:, 0:FF] * scale
-    hidden_all[chip] = (gate / (1.0 + jnp.exp(-gate)) * (up_sum[:, 0:FF] * scale)).astype(BF16)
-
-    own_hidden = hidden_all.at[chip]
-
-    def hid_copy(d):
-        return remote(own_hidden, own_hidden, hid_s.at[d], hid_r.at[d], row, chip_at(d) * 2 + core)
-
-    start(1, CHIPS, hid_copy)
+    pending.extend([wh_swap] + held)
+
+    def hid_copy(i):
+        own_hidden = hidden_all.at[chip, :, CHUNKS[i][0]:CHUNKS[i][0] + HALF]
+
+        def copy(d):
+            return remote(own_hidden, own_hidden, hid_s.at[i, d], hid_r.at[i, d], row, chip_at(d) * 2 + core)
+
+        return copy
+
+    hidden_all[chip, :, FF:FFP] = jnp.zeros((32, FFP - FF), BF16)
+    for i, (low, width) in enumerate(CHUNKS):
+        arrive(1, CHIPS, gu_copy(i))
+        total = jnp.sum(gu_recv[i].astype(F32), axis=0)
+        if i == 0:
+            scale = inverse_rms(total[:, width:width + 1] + total[:, HALF + width:HALF + width + 1])
+        gate = total[:, 0:width] * scale
+        hidden = gate / (1.0 + jnp.exp(-gate)) * (total[:, HALF:HALF + width] * scale)
+        hidden_all[chip, :, low:low + width] = hidden.astype(BF16)
+        start(1, CHIPS, hid_copy(i))
     ready("wd")
-    arrive(1, CHIPS, hid_copy)
-
-    hidden = hidden_all[...].reshape(T, FF)
-    down_send[...] = dot_nt(hidden, wd[...]).reshape(ROWS, 32, CHIP)
+
+    product = jnp.zeros((T, CHIP), F32)
+    for i, (low, width) in enumerate(CHUNKS):
+        arrive(1, CHIPS, hid_copy(i))
+        hidden = hidden_all[:, :, low:low + width].reshape(T, width)
+        product += dot_nt(hidden, wd[:, low:low + width])
+    down_send[...] = product.reshape(ROWS, 32, CHIP)
 
     def down_copy(d):
         r = row_at(d)
@@ -359,12 +372,12 @@
     orders = ("zyx", "xzy", "yxz")
 
     def axis_copies(p, stage):
-        order = orders[p]
+        order = orders[p % 3]
         axis, done = order[stage], order[:stage]
         one = {"y": pl.ds(cy, 1), "x": pl.ds(cx, 1), "zl": pl.ds(zl, 1), "zh": pl.ds(zh, 1)}
         full = {"y": pl.ds(0, 4), "x": pl.ds(0, 4), "zl": pl.ds(0, 2), "zh": pl.ds(0, 2)}
         pick = {k: full[k] if k[0] in done else one[k] for k in one}
-        ref = parts[p].at[pick["y"], pick["zl"], pick["x"], pick["zh"]]
+        ref = parts[p % 3].at[pick["y"], pick["zl"], pick["x"], pick["zh"], pl.ds(p // 3 * 16, 16)]
         copies = []
         for d in (2, 1, 3):
             x = lax.rem(cx + d, 4) if axis == "x" else cx
@@ -375,23 +388,24 @@
             copies.append(remote(ref, ref, fin_s.at[i], fin_r.at[i], r, c))
         return copies
 
-    gathers = [[axis_copies(p, stage) for p in range(3)] for stage in range(3)]
+    gathers = [[axis_copies(p, stage) for p in range(6)] for stage in range(3)]
     for stage in range(3):
-        for p in range(3):
+        for p in range(6):
             if stage:
                 for copy in gathers[stage - 1][p]:
                     copy.wait_recv()
             for copy in gathers[stage][p]:
                 copy.start()
                 pending.append(copy.wait_send)
-    last = pending[-9:]
-    del pending[-9:]
+    last = pending[-18:]
+    del pending[-18:]
     flush()
     pending.extend(last)
     ready("wh")
+    ready("targets")
     diagonal = lax.broadcasted_iota(jnp.int32, (T, T), 0) == lax.broadcasted_iota(jnp.int32, (T, T), 1)
-    target = jnp.sum(jnp.where(diagonal, targets[...].astype(F32), 0.0), axis=1, keepdims=True).astype(jnp.int32)
-    for p in range(3):
+    target = jnp.sum(jnp.where(diagonal, target_row[...].astype(F32), 0.0), axis=1, keepdims=True).astype(jnp.int32)
+    for p in range(6):
         for copy in gathers[2][p]:
             copy.wait_recv()
 
@@ -471,9 +485,10 @@
     result = pl.pallas_call(
         kernel,
         out_shape=jax.ShapeDtypeStruct((1, SEQS), F32),
-        in_specs=[anywhere] * 12 + [smem, vmem],
+        in_specs=[anywhere] * 12 + [smem, anywhere],
         out_specs=vmem,
         scratch_shapes=[
+            pltpu.VMEM((1, T), jnp.int32),
             pltpu.VMEM((2, 32, FEAT), BF16),
             pltpu.VMEM((COLS, 8, HEAD), F32),
             pltpu.VMEM((ROWS, 32, FEAT), BF16),
@@ -497,11 +512,9 @@
             pltpu.VMEM((ROWS, 16, CHIP), F32),
             pltpu.VMEM((ROWS, 16, CHIP), F32),
             pltpu.VMEM((ROWS, 2, 16, CHIP), BF16),
+            pltpu.VMEM((2, CHIPS, 32, FFP), BF16),
+            pltpu.VMEM((2, CHIPS, 32, FFP), BF16),
             pltpu.VMEM((CHIPS, 32, FFP), BF16),
-            pltpu.VMEM((CHIPS, 32, FFP), BF16),
-            pltpu.VMEM((CHIPS, 32, FFP), BF16),
-            pltpu.VMEM((CHIPS, 32, FFP), BF16),
-            pltpu.VMEM((CHIPS, 32, FF), BF16),
             pltpu.VMEM((ROWS, 32, CHIP), F32),
             pltpu.VMEM((ROWS, 32, CHIP), F32),
             pltpu.VMEM((4, 2, 4, 2, 32, 256), BF16),
@@ -511,7 +524,7 @@
             pltpu.VMEM((8, T), F32),
             pltpu.VMEM((CHIPS, 8, T), F32),
             pltpu.VMEM((2, ROWS, 8, T), F32),
-            dma((12,)), dma((8,)), dma((8,)),
+            dma((13,)), dma((8,)), dma((8,)),
             dma((COLS,)), dma((COLS,)),
             dma((ROWS,)), dma((ROWS,)),
             dma, dma,
@@ -520,9 +533,9 @@
             dma((ROWS,)), dma((ROWS,)),
             dma((2 * ROWS,)), dma((2 * ROWS,)),
             dma((2, CHIPS)), dma((2, CHIPS)),
-            dma((CHIPS,)), dma((CHIPS,)),
+            dma((2, CHIPS)), dma((2, CHIPS)),
             dma((ROWS,)), dma((ROWS,)),
-            dma((27,)), dma((27,)),
+            dma((54,)), dma((54,)),
             dma((CHIPS,)), dma((CHIPS,)),
             dma((2 * ROWS,)), dma((2 * ROWS,)),
         ],

time: 143 us -> 140 us (0.979)
  Pallas kernels: 142 us -> 138 us
    pallas_call x1, Pallas kernels: 142 us -> 138 us  [per_device(): pl.pallas_call(kernel, out_shape=jax.ShapeDtypeStruct((1, SEQS), F32), in...]
where the time goes in v4:
time: 140 us; the launch traced here: 139 us
  Pallas kernels  138 us (99%)
    pallas_call x1, Pallas kernels, per_device(): pl.pallas_call(kernel, out_shape=jax.ShapeDtypeStruct((1, SEQS), F32), in...  138 us

profile of v4, /device:TPU:1, one launch (start us, length us, event | category | flops | bytes accessed | tf_op | source)
XLA Modules:
  0.0 139.5 jit_solution(9683432964694313853)
XLA Ops:
  0.0 138.3 %shard_map.136 = f32[1,8]{1,0:T(1,128)} custom-call(bf16[32,320]{1,0:T(8,128)(2,1)} %res.1, f32[320]{0:T(512)} %attn_gain.1, bf16[320,640]{1,0:T(8,128)(2,1)} %w_query.1, bf16[320,128]{1,0:T(8,128)(2,1)} %w_key.1, bf16[320,128]{1,0:T(8,128)(2,1)} %w_value.1, bf16[320,640]{1,0:T(8,128)(2,1)} %bitcast.5, f32[320]{0:T(512)} %mlp_gain.1, ...), custom_call_target="tpu_custom_call" | custom-call | tf_op jit(solution)/shard_map/pallas_call | solution.py:485
  138.3 1.2 copy.16

commit v5 on v4

--- a/solution.py
+++ b/solution.py
@@ -51,14 +51,17 @@
     return lax.dot_general(a, b, (((1,), (1,)), ((), ())), preferred_element_type=F32)
 
 
-def split_sum(total, width):
-    high = total.astype(BF16)
-    low = (total - high.astype(F32)).astype(BF16)
-    shape = (total.shape[0], width)
-    return (
-        jnp.broadcast_to(high.astype(F32), shape).astype(BF16),
-        jnp.broadcast_to(low.astype(F32), shape).astype(BF16),
-    )
+def diagonal_of(count):
+    return lax.broadcasted_iota(jnp.int32, (count, HEAD), 0) == lax.broadcasted_iota(jnp.int32, (count, HEAD), 1)
+
+
+def to_row(column):
+    row = jnp.sum(jnp.where(diagonal_of(column.shape[0]), column, 0.0), axis=0, keepdims=True)
+    return jnp.broadcast_to(row, (8, HEAD))
+
+
+def to_column(rows, count):
+    return jnp.sum(jnp.where(diagonal_of(count), rows[0:1], 0.0), axis=1, keepdims=True)
 
 
 def inverse_rms(total):
@@ -82,11 +85,11 @@
     res, attn_gain, w_query, w_key, w_value, w_out, mlp_gain, w_gate, w_up, w_down, final_gain, w_head, lens, targets,
     out,
     target_row, res_chip, square_all, x_all, wqkv, wo, wg, wu, wd, wh, gain_a, gain_m, gain_f, mg, fg,
-    part_own, part_pair, part_send, part_recv, qkv_all, attended, proj_send, proj_recv, stream_all,
-    gu_send, gu_recv, hidden_all, down_send, down_recv,
+    part_own, part_pair, part_send, part_recv, qkv_all, attended, proj_send, proj_recv, stream_chip, norm_all, mlp_all,
+    gu_own, gu_send, gu_z0, gu_y0, gu_z1, gu_y1, mid_own, mid_send, mid2_own, mid2_send, hidden_all, down_send, down_recv,
     fin_a, fin_b, fin_c, logits, stat_send, stat_recv, stat2_recv,
     local_sem, swap_send, swap_recv, sq_s, sq_r, x_s, x_r, pair_s, pair_r, part_s, part_r, qkv_s, qkv_r, proj_s, proj_r,
-    stream_s, stream_r, gu_s, gu_r, hid_s, hid_r, down_s, down_r, fin_s, fin_r, st_s, st_r, st2_s, st2_r,
+    norm_s, norm_r, stream_s, stream_r, y_s, y_r, z_s, z_r, down_s, down_r, fin_s, fin_r, st_s, st_r, st2_s, st2_r,
 ):
     row, col = lax.axis_index("row"), lax.axis_index("col")
     core = lax.rem(col, 2)
@@ -167,9 +170,7 @@
 
     ready("residual", "gains")
     x = res_chip[core].astype(F32)
-    eye = lax.broadcasted_iota(jnp.int32, (32, HEAD), 0) == lax.broadcasted_iota(jnp.int32, (32, HEAD), 1)
-    square = jnp.sum(jnp.where(eye, jnp.sum(x * x, axis=1, keepdims=True), 0.0), axis=0, keepdims=True)
-    square_all[0] = jnp.broadcast_to(square, (8, HEAD))
+    square_all[0] = to_row(jnp.sum(x * x, axis=1, keepdims=True))
 
     def sq_copy(d):
         return remote(square_all.at[0], square_all.at[d], sq_s.at[d], sq_r.at[d], row, col_at(d))
@@ -188,8 +189,7 @@
     sine = jnp.where(low_half, -jnp.sin(angle), jnp.sin(angle))
 
     arrive(1, COLS, sq_copy)
-    square = jnp.sum(square_all[...], axis=0)[0:1]
-    square = jnp.sum(jnp.where(eye, square, 0.0), axis=1, keepdims=True)
+    square = to_column(jnp.sum(square_all[...], axis=0), 32)
     x_all[row] = (x * inverse_rms(square) * gain_a[...].reshape(1, FEAT)).astype(BF16)
 
     def x_copy(d):
@@ -278,9 +278,29 @@
     arrive(1, ROWS, proj_copy)
     half_rows = pl.ds(pl.multiple_of(core * 16, 16), 16)
     residual = jnp.concatenate([res_chip[0, half_rows, :], res_chip[1, half_rows, :]], axis=1).astype(F32)
-    stream_all[row, core] = (residual + jnp.sum(proj_recv[...], axis=0)).astype(BF16)
-
-    own_stream = stream_all.at[row, core]
+    stream = (residual + jnp.sum(proj_recv[...], axis=0)).astype(BF16)
+    stream_chip[core] = stream
+    stream = stream.astype(F32)
+
+    def norm(i, value, gain):
+        count = value.shape[0]
+        norm_all[i, 0] = to_row(jnp.sum(value * value, axis=1, keepdims=True))
+
+        def copy(d):
+            return remote(
+                norm_all.at[i, 0], norm_all.at[i, d], norm_s.at[i, d], norm_r.at[i, d], row, chip_at(d) * 2 + core
+            )
+
+        start(1, CHIPS, copy)
+        arrive(1, CHIPS, copy)
+        square = to_column(jnp.sum(norm_all[i], axis=0), count)
+        gain = jnp.concatenate([gain[0], gain[1]], axis=1)
+        return (value * inverse_rms(square) * gain).astype(BF16)
+
+    ready("gains_pair")
+    mlp_all[row, core] = norm(0, stream, mg)
+
+    own_stream = mlp_all.at[row, core]
 
     def stream_copy(d):
         return remote(own_stream, own_stream, stream_s.at[d], stream_r.at[d], row_at(d), col)
@@ -290,64 +310,101 @@
 
     start(1, ROWS, stream_copy)
     start(0, ROWS, stream_cross)
+    swap("stream_pair", stream_chip.at[core], stream_chip.at[core])
     own("wh", w_head, wh.at[core])
     swap("wh", w_head, wh.at[core])
     wh_at = len(pending) - 1
-    ready("wg", "wu", "gains_pair")
+    ready("wg", "wu")
     arrive(1, ROWS, stream_copy)
     arrive(0, ROWS, stream_cross)
 
-    stream = stream_all[...].reshape(T, CHIP).astype(F32)
-    square_hi, square_lo = split_sum(jnp.sum(stream * stream, axis=1, keepdims=True), HALF - CHUNKS[0][1])
-    gain = jnp.concatenate([mg[0], mg[1]], axis=1)
-    xg = (stream * gain).astype(BF16)
-
-    def gu_copy(i):
+    mlp_in = mlp_all[...].reshape(T, CHIP)
+
+    def y_peer(d):
+        return (lax.rem(cy + d, 4) * 2 + zl) * 2 + core
+
+    z_peer = (cy * 2 + 1 - zl) * 2 + core
+
+    def to_y(src, dst, i):
         def copy(d):
-            c = chip_at(d)
-            return remote(gu_send.at[i, c], gu_recv.at[i, d], gu_s.at[i, d], gu_r.at[i, d], row, c * 2 + core)
+            return remote(src(lax.rem(cy + d, 4)), dst(d), y_s.at[i, d], y_r.at[i, d], row, y_peer(d))
 
         return copy
 
-    for i, (low, width) in enumerate(CHUNKS):
+    def to_z(src, dst, i):
+        return lambda d: remote(src, dst, z_s.at[i], z_r.at[i], row, z_peer)
+
+    def gate_up(i):
+        low, width = CHUNKS[i]
         for half, weight in enumerate((wg, wu)):
-            product = jnp.dot(xg, weight[:, low:low + width], preferred_element_type=F32)
-            gu_send[i, :, :, half * HALF:half * HALF + width] = product.astype(BF16).reshape(CHIPS, 32, width)
-        if i == 0:
-            gu_send[0, :, :, width:HALF] = square_hi.reshape(CHIPS, 32, HALF - width)
-            gu_send[0, :, :, HALF + width:FFP] = square_lo.reshape(CHIPS, 32, HALF - width)
-        start(1, CHIPS, gu_copy(i))
-        gu_recv[i, 0] = gu_send[i, chip]
+            product = jnp.dot(mlp_in, weight[:, low:low + width], preferred_element_type=F32)
+            product = product.reshape(4, 2, 32, width)
+            gu_own[i, :, :, :, half * HALF:half * HALF + width] = product
+            gu_send[i, :, :, :, half * HALF:half * HALF + width] = product.astype(BF16)
+            if width < HALF:
+                rest = jnp.zeros((4, 2, 32, HALF - width), F32)
+                gu_own[i, :, :, :, half * HALF + width:(half + 1) * HALF] = rest
+                gu_send[i, :, :, :, half * HALF + width:(half + 1) * HALF] = rest.astype(BF16)
+
+    gate_up(0)
+    sum_z0 = to_z(gu_send.at[0, :, 1 - zl], gu_z0, 0)
+    start(0, 1, sum_z0)
+    gate_up(1)
+    sum_y1 = to_y(lambda y: gu_send.at[1, y], lambda d: gu_y1.at[d], 0)
+    start(1, 4, sum_y1)
     held = pending[-2:]
     del pending[-2:]
     wh_swap = pending.pop(wh_at)
     flush()
     pending.extend([wh_swap] + held)
 
-    def hid_copy(i):
-        own_hidden = hidden_all.at[chip, :, CHUNKS[i][0]:CHUNKS[i][0] + HALF]
-
-        def copy(d):
-            return remote(own_hidden, own_hidden, hid_s.at[i, d], hid_r.at[i, d], row, chip_at(d) * 2 + core)
-
-        return copy
-
-    hidden_all[chip, :, FF:FFP] = jnp.zeros((32, FFP - FF), BF16)
-    for i, (low, width) in enumerate(CHUNKS):
-        arrive(1, CHIPS, gu_copy(i))
-        total = jnp.sum(gu_recv[i].astype(F32), axis=0)
-        if i == 0:
-            scale = inverse_rms(total[:, width:width + 1] + total[:, HALF + width:HALF + width + 1])
-        gate = total[:, 0:width] * scale
-        hidden = gate / (1.0 + jnp.exp(-gate)) * (total[:, HALF:HALF + width] * scale)
-        hidden_all[chip, :, low:low + width] = hidden.astype(BF16)
-        start(1, CHIPS, hid_copy(i))
+    arrive(0, 1, sum_z0)
+    mid_own[...] = gu_own[0, :, zl] + gu_z0[...].astype(F32)
+    mid_send[...] = mid_own[...].astype(BF16)
+    sum_y0 = to_y(lambda y: mid_send.at[y], lambda d: gu_y0.at[d], 1)
+    start(1, 4, sum_y0)
+    arrive(1, 4, sum_y1)
+    gu_y1[0] = jnp.zeros((2, 32, FFP), BF16)
+    mid2_own[...] = gu_own[1, cy] + jnp.sum(gu_y1[...].astype(F32), axis=0)
+    mid2_send[...] = mid2_own[1 - zl].astype(BF16)
+    sum_z1 = to_z(mid2_send, gu_z1, 1)
+    start(0, 1, sum_z1)
+
+    def activate(i, total):
+        low, width = CHUNKS[i]
+        gate = total[:, 0:width]
+        hidden = gate / (1.0 + jnp.exp(-gate)) * total[:, HALF:HALF + width]
+        hidden_all[cy, zl, :, low:low + width] = hidden.astype(BF16)
+
+    def lanes(i):
+        return pl.ds(CHUNKS[i][0], HALF)
+
+    hidden_all[cy, zl, :, FF:FFP] = jnp.zeros((32, FFP - FF), BF16)
+    arrive(1, 4, sum_y0)
+    gu_y0[0] = jnp.zeros((32, FFP), BF16)
+    activate(0, mid_own[cy] + jnp.sum(gu_y0[...].astype(F32), axis=0))
+    own0 = hidden_all.at[cy, zl, :, lanes(0)]
+    hid_z0 = to_z(own0, own0, 2)
+    start(0, 1, hid_z0)
+    arrive(0, 1, sum_z1)
+    activate(1, mid2_own[zl] + gu_z1[...].astype(F32))
+    own1 = hidden_all.at[cy, zl, :, lanes(1)]
+    hid_y1 = to_y(lambda y: own1, lambda d: own1, 2)
+    start(1, 4, hid_y1)
+    arrive(0, 1, hid_z0)
+    both0 = hidden_all.at[cy, :, :, lanes(0)]
+    hid_y0 = to_y(lambda y: both0, lambda d: both0, 3)
+    start(1, 4, hid_y0)
+    arrive(1, 4, hid_y1)
+    four1 = hidden_all.at[:, zl, :, lanes(1)]
+    hid_z1 = to_z(four1, four1, 3)
+    start(0, 1, hid_z1)
     ready("wd")
 
     product = jnp.zeros((T, CHIP), F32)
     for i, (low, width) in enumerate(CHUNKS):
-        arrive(1, CHIPS, hid_copy(i))
-        hidden = hidden_all[:, :, low:low + width].reshape(T, width)
+        arrive(*((1, 4, hid_y0) if i == 0 else (0, 1, hid_z1)))
+        hidden = hidden_all[:, :, :, low:low + width].reshape(T, width)
         product += dot_nt(hidden, wd[:, low:low + width])
     down_send[...] = product.reshape(ROWS, 32, CHIP)
 
@@ -358,15 +415,13 @@
     start(1, ROWS, down_copy)
     down_recv[0] = down_send[row]
     arrive(1, ROWS, down_copy)
-    final = stream_all[row].reshape(32, CHIP).astype(F32) + jnp.sum(down_recv[...], axis=0)
-    square_hi, square_lo = split_sum(jnp.sum(final * final, axis=1, keepdims=True), 64)
-    final = (final * jnp.concatenate([fg[0], fg[1]], axis=1)).astype(BF16)
+    ready("stream_pair")
+    final = stream_chip[...].reshape(32, CHIP).astype(F32) + jnp.sum(down_recv[...], axis=0)
+    final = norm(1, final, fg)
 
     fin_a[cy, zl, cx, zh] = final[:, 0:256]
     fin_b[cy, zl, cx, zh] = final[:, 256:512]
-    fin_c[cy, zl, cx, zh, :, 0:128] = final[:, 512:640]
-    fin_c[cy, zl, cx, zh, :, 128:192] = square_hi
-    fin_c[cy, zl, cx, zh, :, 192:256] = square_lo
+    fin_c[cy, zl, cx, zh] = final[:, 512:640]
 
     parts = (fin_a, fin_b, fin_c)
     orders = ("zyx", "xzy", "yxz")
@@ -409,19 +464,15 @@
         for copy in gathers[2][p]:
             copy.wait_recv()
 
-    square = jnp.zeros((T, 1), F32)
     for y in range(4):
         pieces = []
         for z in range(2):
-            c = fin_c[y, z].reshape(T, 256)
-            square = square + c[:, 128:129].astype(F32) + c[:, 192:193].astype(F32)
-            pieces += [fin_a[y, z].reshape(T, 256), fin_b[y, z].reshape(T, 256), c[:, 0:128]]
+            pieces += [fin_a[y, z].reshape(T, 256), fin_b[y, z].reshape(T, 256), fin_c[y, z].reshape(T, HEAD)]
         states = jnp.concatenate(pieces, axis=1)
         for j in range(2):
             product = jnp.dot(states, wh[j, y * 2 * CHIP:(y + 1) * 2 * CHIP], preferred_element_type=F32)
             logits[j] = product if y == 0 else logits[j] + product
-    scale = inverse_rms(square)
-    both = [logits[j] * scale for j in range(2)]
+    both = [logits[j] for j in range(2)]
     top = jnp.maximum(*[jnp.max(l, axis=1, keepdims=True) for l in both])
     exponential = sum(jnp.sum(jnp.exp(l - top), axis=1, keepdims=True) for l in both)
     picked = jnp.zeros((T, 1), F32)
@@ -431,35 +482,48 @@
         picked = picked + jnp.sum(jnp.where(ids == target, both[j], 0.0), axis=1, keepdims=True)
     lane = lax.broadcasted_iota(jnp.int32, (T, HEAD), 1)
     packed = jnp.where(lane == 0, top, jnp.where(lane == 1, exponential, picked))
-    stat_recv[0] = jnp.transpose(packed)[0:8, :]
-
-    def st_copy(d):
-        return remote(stat_recv.at[0], stat_recv.at[d], st_s.at[d], st_r.at[d], row, chip_at(d) * 2 + core)
-
-    start(1, CHIPS, st_copy)
-    arrive(1, CHIPS, st_copy)
+    stat_recv[0, 0] = jnp.transpose(packed)[0:8, :]
 
     def merge(blocks):
         top = jnp.max(blocks[:, 0:1, :], axis=0)
         exponential = jnp.sum(blocks[:, 1:2, :] * jnp.exp(blocks[:, 0:1, :] - top[None]), axis=0)
         return top, exponential, jnp.sum(blocks[:, 2:3, :], axis=0)
 
-    top, exponential, picked = merge(stat_recv[...])
     line = lax.broadcasted_iota(jnp.int32, (8, T), 0)
-    stat_send[...] = jnp.where(line == 0, top, jnp.where(line == 1, exponential, picked))
-    own_stat = stat2_recv.at[core, row]
-    stat2_recv[core, row] = stat_send[...]
+
+    def packed_merge(blocks):
+        top, exponential, picked = merge(blocks)
+        return jnp.where(line == 0, top, jnp.where(line == 1, exponential, picked))
+
+    for stage in range(2):
+        def st_copy(d):
+            if stage == 0:
+                r, c = at_xyz(cx, cy, lax.rem(cz + d, 4))
+            else:
+                r, c = at_xyz(cx, lax.rem(cy + d, 4), cz)
+            return remote(stat_recv.at[stage, 0], stat_recv.at[stage, d], st_s.at[stage, d], st_r.at[stage, d], r, c)
+
+        each(1, 4, lambda d: st_copy(d).start())
+        arrive(1, 4, st_copy)
+        each(1, 4, lambda d: st_copy(d).wait_send())
+        merged = packed_merge(stat_recv[stage])
+        if stage == 0:
+            stat_recv[1, 0] = merged
+        else:
+            stat_send[...] = merged
+            stat2_recv[core, cx] = merged
+    own_stat = stat2_recv.at[core, cx]
 
     def st2_copy(d):
-        return remote(stat_send, own_stat, st2_s.at[d], st2_r.at[d], row_at(d), col)
+        return remote(stat_send, own_stat, st2_s.at[d], st2_r.at[d], lax.rem(cx + d, 4) * 2 + zh, col)
 
     def st2_cross(d):
-        return remote(stat_send, own_stat, st2_s.at[ROWS + d], st2_r.at[ROWS + d], row_at(d), sib)
-
-    start(1, ROWS, st2_copy)
-    start(0, ROWS, st2_cross)
-    arrive(1, ROWS, st2_copy)
-    arrive(0, ROWS, st2_cross)
+        return remote(stat_send, own_stat, st2_s.at[4 + d], st2_r.at[4 + d], lax.rem(cx + d, 4) * 2 + zh, sib)
+
+    start(1, 4, st2_copy)
+    start(0, 4, st2_cross)
+    arrive(1, 4, st2_copy)
+    arrive(0, 4, st2_cross)
     logprob = []
     for m in range(2):
         top, exponential, picked = merge(stat2_recv[m])
@@ -511,33 +575,44 @@
             pltpu.VMEM((T // 2, QW), BF16),
             pltpu.VMEM((ROWS, 16, CHIP), F32),
             pltpu.VMEM((ROWS, 16, CHIP), F32),
+            pltpu.VMEM((2, 16, CHIP), BF16),
+            pltpu.VMEM((2, CHIPS, 8, HEAD), F32),
             pltpu.VMEM((ROWS, 2, 16, CHIP), BF16),
-            pltpu.VMEM((2, CHIPS, 32, FFP), BF16),
-            pltpu.VMEM((2, CHIPS, 32, FFP), BF16),
-            pltpu.VMEM((CHIPS, 32, FFP), BF16),
+            pltpu.VMEM((2, 4, 2, 32, FFP), F32),
+            pltpu.VMEM((2, 4, 2, 32, FFP), BF16),
+            pltpu.VMEM((4, 32, FFP), BF16),
+            pltpu.VMEM((4, 32, FFP), BF16),
+            pltpu.VMEM((32, FFP), BF16),
+            pltpu.VMEM((4, 2, 32, FFP), BF16),
+            pltpu.VMEM((4, 32, FFP), F32),
+            pltpu.VMEM((4, 32, FFP), BF16),
+            pltpu.VMEM((2, 32, FFP), F32),
+            pltpu.VMEM((32, FFP), BF16),
+            pltpu.VMEM((4, 2, 32, FFP), BF16),
             pltpu.VMEM((ROWS, 32, CHIP), F32),
             pltpu.VMEM((ROWS, 32, CHIP), F32),
             pltpu.VMEM((4, 2, 4, 2, 32, 256), BF16),
             pltpu.VMEM((4, 2, 4, 2, 32, 256), BF16),
-            pltpu.VMEM((4, 2, 4, 2, 32, 256), BF16),
+            pltpu.VMEM((4, 2, 4, 2, 32, HEAD), BF16),
             pltpu.VMEM((2, T, VOCAB), F32),
             pltpu.VMEM((8, T), F32),
-            pltpu.VMEM((CHIPS, 8, T), F32),
-            pltpu.VMEM((2, ROWS, 8, T), F32),
-            dma((13,)), dma((8,)), dma((8,)),
+            pltpu.VMEM((2, 4, 8, T), F32),
+            pltpu.VMEM((2, 4, 8, T), F32),
+            dma((13,)), dma((9,)), dma((9,)),
             dma((COLS,)), dma((COLS,)),
             dma((ROWS,)), dma((ROWS,)),
             dma, dma,
             dma((CHIPS,)), dma((CHIPS,)),
             dma((COLS,)), dma((COLS,)),
             dma((ROWS,)), dma((ROWS,)),
+            dma((2, CHIPS)), dma((2, CHIPS)),
             dma((2 * ROWS,)), dma((2 * ROWS,)),
-            dma((2, CHIPS)), dma((2, CHIPS)),
-            dma((2, CHIPS)), dma((2, CHIPS)),
+            dma((4, 4)), dma((4, 4)),
+            dma((4,)), dma((4,)),
             dma((ROWS,)), dma((ROWS,)),
             dma((54,)), dma((54,)),
+            dma((2, 4)), dma((2, 4)),
             dma((CHIPS,)), dma((CHIPS,)),
-            dma((2 * ROWS,)), dma((2 * ROWS,)),
         ],
         compiler_params=pltpu.CompilerParams(
             collective_id=0, has_side_effects=True, vmem_limit_bytes=60 * 1024 * 1024

time: 140 us -> 139 us (level)
  no operation moved by 1% of the time
where the time goes in v5:
time: 139 us
  Pallas kernels  138 us (99%)
    pallas_call x1, Pallas kernels, per_device(): pl.pallas_call(kernel, out_shape=jax.ShapeDtypeStruct((1, SEQS), F32), in...  138 us

profile of v5, /device:TPU:1, one launch (start us, length us, event | category | flops | bytes accessed | tf_op | source)
XLA Modules:
  0.0 139.1 jit_solution(16125696642743629931)
XLA Ops:
  0.0 137.9 %shard_map.136 = f32[1,8]{1,0:T(1,128)} custom-call(bf16[32,320]{1,0:T(8,128)(2,1)} %res.1, f32[320]{0:T(512)} %attn_gain.1, bf16[320,640]{1,0:T(8,128)(2,1)} %w_query.1, bf16[320,128]{1,0:T(8,128)(2,1)} %w_key.1, bf16[320,128]{1,0:T(8,128)(2,1)} %w_value.1, bf16[320,640]{1,0:T(8,128)(2,1)} %bitcast.5, f32[320]{0:T(512)} %mlp_gain.1, ...), custom_call_target="tpu_custom_call" | custom-call | tf_op jit(solution)/shard_map/pallas_call | solution.py:549
  137.9 1.2 copy.16

commit v6 on v5

v6 whole, which is shorter than its diff:
```python
import math

import jax
import jax.numpy as jnp
from jax import lax
from jax.experimental import pallas as pl
from jax.experimental.pallas import tpu as pltpu
from jax.sharding import PartitionSpec as P

T = 256
D = 5120
HEAD = 128
Q_HEADS = 5
QW = Q_HEADS * HEAD
QKV = QW + 2 * HEAD
SEQS = 8
FEAT = 320
CHIP = 2 * FEAT
FF = 1728
FFP = 1792
HALF = FFP // 2
CHUNKS = ((HALF, FF - HALF), (0, HALF))
VOCAB = 640
ROWS = 8
COLS = 16
CHIPS = 8
EPSILON = 1e-06
ROPE_BASE = 1000000.0
MASKED = -1e30
MESH = pl.DeviceIdType.MESH
F32 = jnp.float32
BF16 = jnp.bfloat16


def remote(src, dst, send, recv, row, col):
    return pltpu.make_async_remote_copy(
        src_ref=src, dst_ref=dst, send_sem=send, recv_sem=recv,
        device_id={"row": row, "col": col}, device_id_type=MESH,
    )


def dot_nt(a, b):
    return lax.dot_general(a, b, (((1,), (1,)), ((), ())), preferred_element_type=F32)


def diagonal_of(count):
    return lax.broadcasted_iota(jnp.int32, (count, HEAD), 0) == lax.broadcasted_iota(jnp.int32, (count, HEAD), 1)


def to_row(column):
    row = jnp.sum(jnp.where(diagonal_of(column.shape[0]), column, 0.0), axis=0, keepdims=True)
    return jnp.broadcast_to(row, (8, HEAD))


def to_column(rows, count):
    return jnp.sum(jnp.where(diagonal_of(count), rows[0:1], 0.0), axis=1, keepdims=True)


def inverse_rms(total):
    return lax.rsqrt(total / D + EPSILON)


def layout_of(lens_ref, token):
    segment = jnp.zeros_like(token)
    start = jnp.zeros_like(token)
    end = jnp.int32(0)
    for s in range(SEQS):
        length = lens_ref[s]
        end = end + length
        before = end <= token
        segment = segment + jnp.where(before, 1, 0)
        start = start + jnp.where(before, length, 0)
    return segment, token - start


def kernel(
    res, attn_gain, w_query, w_key, w_value, w_out, mlp_gain, w_gate, w_up, w_down, final_gain, w_head, lens, targets,
    out,
    target_row, res_chip, tiny, x_all, wqkv, wo, wg, wu, wd, wh, gain_a, gain_m, gain_f, mg, fg,
    part_own, part_pair, part_send, part_r1, part_mid, part_r2, qkv_all, attended,
    proj_send, proj_r1, proj_mid, proj_r2, stream_chip, mlp_all,
    gu_own, gu_send, gu_z0, gu_y0, gu_z1, gu_y1, mid_own, mid_send, mid2_own, mid2_send, hidden_all,
    down_send, down_r1, down_mid, down_r2, fin_a, fin_b, fin_c, logits, stat_recv, stat_all,
    local_sem, send_sem, recv_sem,
):
    row, col = lax.axis_index("row"), lax.axis_index("col")
    core = lax.rem(col, 2)
    other = 1 - core
    chip = lax.div(col, 2)
    cx, zh = lax.div(row, 2), lax.rem(row, 2)
    cy, zl = lax.div(chip, 2), lax.rem(chip, 2)
    cz = zh * 2 + zl
    sib = chip * 2 + other

    place = {"x": cx, "y": cy, "z": cz, "zl": zl, "zh": zh, "core": core}
    size = {"x": 4, "y": 4, "z": 4, "zl": 2, "zh": 2, "core": 2}

    def peer(axis, d):
        at = dict(place)
        at[axis] = lax.rem(at[axis] + d, size[axis])
        z = at["z"] if axis == "z" else at["zh"] * 2 + at["zl"]
        device = at["x"] * 2 + lax.div(z, 2), (at["y"] * 2 + lax.rem(z, 2)) * 2 + at["core"]
        return at[axis], device

    mine = pl.ds(pl.multiple_of(core * FEAT, 64), FEAT)
    waits, pending, numbers = {}, [], {"own": 0, "sent": 0}

    def own(name, src, dst):
        copy = pltpu.make_async_copy(src, dst, local_sem.at[numbers["own"]])
        numbers["own"] += 1
        copy.start()
        waits.setdefault(name, []).append(copy.wait)

    def one(axis, d, src, dst):
        i = numbers["sent"]
        numbers["sent"] += 1
        copy = remote(src, dst, send_sem.at[i], recv_sem.at[i], *peer(axis, d)[1])
        copy.start()
        pending.append(copy.wait_send)
        return copy

    def send(axis, src, dst):
        return [one(axis, d, src(peer(axis, d)[0]), dst(d)) for d in range(1, size[axis])]

    def spread(axis, ref):
        return send(axis, lambda at: ref, lambda d: ref)

    def arrive(copies):
        for copy in copies:
            copy.wait_recv()

    def swap(name, src, dst):
        waits.setdefault(name, []).append(one("core", 1, src, dst).wait_recv)

    def ready(*names):
        for name in names:
            for wait in waits.pop(name):
                wait()

    def flush(count):
        for finish in pending[:count]:
            finish()
        del pending[:count]

    def reduce(blocks, first, second, arrived, middle, last):
        copies = send(first, lambda at: blocks.at[at], lambda d: arrived.at[d])
        arrived[0] = blocks[place[first]]
        arrive(copies)
        middle[...] = jnp.sum(arrived[...], axis=0)
        arrive(send(second, lambda at: middle.at[at], lambda d: last))
        return middle[place[second]] + last[...]

    def column_sum(i, column, axes):
        value = to_row(column)
        for axis in axes:
            tiny[i, 0] = value
            arrive(send(axis, lambda at: tiny.at[i, 0], lambda d: tiny.at[i, d]))
            value = jnp.sum(tiny[i, 0:size[axis]], axis=0)
            i += 1
        return to_column(value, column.shape[0])

    own("residual", res, res_chip.at[core])
    own("targets", targets, target_row)
    own("gains", attn_gain, gain_a)
    own("gains", mlp_gain, gain_m)
    own("gains", final_gain, gain_f)
    own("wqkv", w_query, wqkv.at[:, 0:QW])
    own("wqkv", w_key, wqkv.at[:, QW:QW + HEAD])
    own("wqkv", w_value, wqkv.at[:, QW + HEAD:QKV])

    barrier = pltpu.get_barrier_semaphore()

    greeted = [("core", 1)] + [(axis, d) for axis in "xyz" for d in (1, 2, 3)]
    for axis, d in greeted:
        r, c = peer(axis, d)[1]
        pl.semaphore_signal(barrier, inc=1, device_id={"row": r, "col": c}, device_id_type=MESH)
    pl.semaphore_wait(barrier, len(greeted))

    ready("residual", "gains")
    x = res_chip[core].astype(F32)
    mg[core] = gain_m[...].reshape(1, FEAT)
    fg[core] = gain_f[...].reshape(1, FEAT)
    square = column_sum(0, jnp.sum(x * x, axis=1, keepdims=True), ("core", "y", "zl"))
    x_all[cx, zh] = (x * inverse_rms(square) * gain_a[...].reshape(1, FEAT)).astype(BF16)
    first = spread("zh", x_all.at[cx, zh])
    swap("residual_pair", res_chip.at[core], res_chip.at[core])
    swap("gains_pair", mg.at[core], mg.at[core])
    swap("gains_pair", fg.at[core], fg.at[core])
    own("wo", w_out, wo.at[mine])
    swap("wo", w_out, wo.at[mine])
    arrive(first)
    second = spread("x", x_all.at[cx])

    own_token = COLS * col + lax.broadcasted_iota(jnp.int32, (16, HEAD), 0)
    position = layout_of(lens, own_token)[1].astype(F32)
    lane = lax.broadcasted_iota(jnp.int32, (16, HEAD), 1)
    low_half = lane < HEAD // 2
    frequency = jnp.exp(jnp.where(low_half, lane, lane - HEAD // 2).astype(F32) * (-2.0 * math.log(ROPE_BASE) / HEAD))
    angle = position * frequency
    cosine = jnp.cos(angle)
    sine = jnp.where(low_half, -jnp.sin(angle), jnp.sin(angle))

    ready("wqkv")
    arrive(second)

    part = jnp.dot(x_all[...].reshape(T, FEAT), wqkv[...], preferred_element_type=F32)
    part_own[...] = part.reshape(4, 2, 2, 16, QKV)
    arrive([one("core", 1, part_own.at[:, :, other], part_pair)])
    part_send[...] = part_own[:, :, core] + part_pair[...]
    own("wg", w_gate.at[core], wg.at[mine])
    own("wu", w_up.at[core], wu.at[mine])
    swap("wg", w_gate.at[other], wg.at[mine])
    swap("wu", w_up.at[other], wu.at[mine])
    total = reduce(part_send, "y", "zl", part_r1, part_mid, part_r2)
    for h in range(Q_HEADS + 1):
        head = total[:, h * HEAD:(h + 1) * HEAD]
        turned = head * cosine + pltpu.roll(head, HEAD // 2, 1) * sine
        qkv_all[cy, zl, core, :, h * HEAD:(h + 1) * HEAD] = turned.astype(BF16)
    qkv_all[cy, zl, core, :, QW + HEAD:QKV] = total[:, QW + HEAD:QKV].astype(BF16)

    first = spread("zl", qkv_all.at[cy, zl, core])
    own("wd", w_down.at[core], wd.at[mine])
    swap("wd", w_down.at[other], wd.at[mine])
    arrive(first)
    second = spread("y", qkv_all.at[cy, :, core])

    row_i = lax.broadcasted_iota(jnp.int32, (T // 2, 1), 0)
    q_token = lax.div(row_i, 16) * 32 + core * 16 + lax.rem(row_i, 16)
    k_token = lax.broadcasted_iota(jnp.int32, (1, T), 1)
    q_segment = layout_of(lens, q_token)[0]
    k_segment = layout_of(lens, k_token)[0]
    allowed = (q_segment == k_segment) & (k_token <= q_token)

    arrive(second)
    pairs = qkv_all.at[:, :, core, :, QW:QKV]
    arrive(spread("core", pairs))

    keys = qkv_all[:, :, :, :, QW:QW + HEAD].reshape(T, HEAD)
    values = qkv_all[:, :, :, :, QW + HEAD:QKV].reshape(T, HEAD)
    for h in range(Q_HEADS):
        query = qkv_all[:, :, core, :, h * HEAD:(h + 1) * HEAD].reshape(T // 2, HEAD)
        scores = dot_nt(query, keys)
        scores = jnp.where(allowed, scores * HEAD ** (-0.5), MASKED)
        weights = jnp.exp(scores - jnp.max(scores, axis=1, keepdims=True))
        weights = (weights / jnp.sum(weights, axis=1, keepdims=True)).astype(BF16)
        result = jnp.dot(weights, values, preferred_element_type=F32)
        attended[:, h * HEAD:(h + 1) * HEAD] = result.astype(BF16)

    ready("wo", "residual_pair")
    proj_send[...] = dot_nt(attended[...], wo[...]).reshape(4, 2, 16, CHIP)

    projected = reduce(proj_send, "x", "zh", proj_r1, proj_mid, proj_r2)
    half_rows = pl.ds(pl.multiple_of(core * 16, 16), 16)
    residual = jnp.concatenate([res_chip[0, half_rows, :], res_chip[1, half_rows, :]], axis=1).astype(F32)
    stream = (residual + projected).astype(BF16)
    stream_chip[core] = stream
    stream = stream.astype(F32)

    def norm(i, value, gain):
        square = column_sum(i, jnp.sum(value * value, axis=1, keepdims=True), ("y", "zl"))
        gain = jnp.concatenate([gain[0], gain[1]], axis=1)
        return (value * inverse_rms(square) * gain).astype(BF16)

    ready("gains_pair")
    mlp_all[cx, zh, core] = norm(3, stream, mg)

    first = spread("zh", mlp_all.at[cx, zh, core])
    swap("stream_pair", stream_chip.at[core], stream_chip.at[core])
    own("wh", w_head, wh.at[core])
    swap("wh", w_head, wh.at[core])
    wh_at = len(pending) - 1
    arrive(first)
    arrive(spread("x", mlp_all.at[cx, :, core]))
    arrive(spread("core", mlp_all.at[:, :, core]))
    ready("wg", "wu")

    mlp_in = mlp_all[...].reshape(T, CHIP)

    def gate_up(i):
        low, width = CHUNKS[i]
        for half, weight in enumerate((wg, wu)):
            product = jnp.dot(mlp_in, weight[:, low:low + width], preferred_element_type=F32)
            product = product.reshape(4, 2, 32, width)
            gu_own[i, :, :, :, half * HALF:half * HALF + width] = product
            gu_send[i, :, :, :, half * HALF:half * HALF + width] = product.astype(BF16)
            if width < HALF:
                rest = jnp.zeros((4, 2, 32, HALF - width), F32)
                gu_own[i, :, :, :, half * HALF + width:(half + 1) * HALF] = rest
                gu_send[i, :, :, :, half * HALF + width:(half + 1) * HALF] = rest.astype(BF16)

    gate_up(0)
    sum_z0 = send("zl", lambda at: gu_send.at[0, :, at], lambda d: gu_z0)
    gate_up(1)
    sum_y1 = send("y", lambda at: gu_send.at[1, at], lambda d: gu_y1.at[d])
    flush(wh_at)

    arrive(sum_z0)
    mid_own[...] = gu_own[0, :, zl] + gu_z0[...].astype(F32)
    mid_send[...] = mid_own[...].astype(BF16)
    sum_y0 = send("y", lambda at: mid_send.at[at], lambda d: gu_y0.at[d])
    arrive(sum_y1)
    gu_y1[0] = jnp.zeros((2, 32, FFP), BF16)
    mid2_own[...] = gu_own[1, cy] + jnp.sum(gu_y1[...].astype(F32), axis=0)
    mid2_send[...] = mid2_own[1 - zl].astype(BF16)
    sum_z1 = send("zl", lambda at: mid2_send, lambda d: gu_z1)

    def activate(i, total):
        low, width = CHUNKS[i]
        gate = total[:, 0:width]
        hidden = gate / (1.0 + jnp.exp(-gate)) * total[:, HALF:HALF + width]
        hidden_all[cy, zl, :, low:low + width] = hidden.astype(BF16)

    def lanes(i):
        return pl.ds(CHUNKS[i][0], HALF)

    hidden_all[cy, zl, :, FF:FFP] = jnp.zeros((32, FFP - FF), BF16)
    arrive(sum_y0)
    gu_y0[0] = jnp.zeros((32, FFP), BF16)
    activate(0, mid_own[cy] + jnp.sum(gu_y0[...].astype(F32), axis=0))
    hid_z0 = spread("zl", hidden_all.at[cy, zl, :, lanes(0)])
    arrive(sum_z1)
    activate(1, mid2_own[zl] + gu_z1[...].astype(F32))
    hid_y1 = spread("y", hidden_all.at[cy, zl, :, lanes(1)])
    arrive(hid_z0)
    hid_y0 = spread("y", hidden_all.at[cy, :, :, lanes(0)])
    arrive(hid_y1)
    hid_z1 = spread("zl", hidden_all.at[:, zl, :, lanes(1)])
    ready("wd")

    product = jnp.zeros((T, CHIP), F32)
    for i, (low, width) in enumerate(CHUNKS):
        arrive(hid_y0 if i == 0 else hid_z1)
        hidden = hidden_all[:, :, :, low:low + width].reshape(T, width)
        product += dot_nt(hidden, wd[:, low:low + width])
    down_send[...] = product.reshape(4, 2, 32, CHIP)
    summed = reduce(down_send, "x", "zh", down_r1, down_mid, down_r2)
    ready("stream_pair")
    final = stream_chip[...].reshape(32, CHIP).astype(F32) + summed
    final = norm(5, final, fg)

    fin_a[cy, zl, cx, zh] = final[:, 0:256]
    fin_b[cy, zl, cx, zh] = final[:, 256:512]
    fin_c[cy, zl, cx, zh] = final[:, 512:640]

    parts = (fin_a, fin_b, fin_c)
    orders = ("zyx", "xzy", "yxz")

    def slab(p, stage):
        done = orders[p % 3][:stage]
        alone = {"y": pl.ds(cy, 1), "zl": pl.ds(zl, 1), "x": pl.ds(cx, 1), "zh": pl.ds(zh, 1)}
        pick = [pl.ds(0, size[k]) if k[0] in done else alone[k] for k in alone]
        return parts[p % 3].at[(*pick, pl.ds(p // 3 * 16, 16))]

    before = len(pending)
    gathers = [None] * 6
    for stage in range(3):
        for p in range(6):
            if stage:
                arrive(gathers[p])
            gathers[p] = spread(orders[p % 3][stage], slab(p, stage))
    flush(before)
    ready("wh")
    ready("targets")
    diagonal = lax.broadcasted_iota(jnp.int32, (T, T), 0) == lax.broadcasted_iota(jnp.int32, (T, T), 1)
    target = jnp.sum(jnp.where(diagonal, target_row[...].astype(F32), 0.0), axis=1, keepdims=True).astype(jnp.int32)
    for copies in gathers:
        arrive(copies)

    for y in range(4):
        pieces = []
        for z in range(2):
            pieces += [fin_a[y, z].reshape(T, 256), fin_b[y, z].reshape(T, 256), fin_c[y, z].reshape(T, HEAD)]
        states = jnp.concatenate(pieces, axis=1)
        for j in range(2):
            product = jnp.dot(states, wh[j, y * 2 * CHIP:(y + 1) * 2 * CHIP], preferred_element_type=F32)
            logits[j] = product if y == 0 else logits[j] + product
    both = [logits[j] for j in range(2)]
    top = jnp.maximum(*[jnp.max(l, axis=1, keepdims=True) for l in both])
    exponential = sum(jnp.sum(jnp.exp(l - top), axis=1, keepdims=True) for l in both)
    picked = jnp.zeros((T, 1), F32)
    for j in range(2):
        first = (row * COLS + chip * 2 + j) * VOCAB
        ids = first + lax.broadcasted_iota(jnp.int32, (T, VOCAB), 1)
        picked = picked + jnp.sum(jnp.where(ids == target, both[j], 0.0), axis=1, keepdims=True)
    lane = lax.broadcasted_iota(jnp.int32, (T, HEAD), 1)
    packed = jnp.where(lane == 0, top, jnp.where(lane == 1, exponential, picked))
    stat_recv[0, 0] = jnp.transpose(packed)[0:8, :]

    def merge(blocks):
        top = jnp.max(blocks[:, 0:1, :], axis=0)
        exponential = jnp.sum(blocks[:, 1:2, :] * jnp.exp(blocks[:, 0:1, :] - top[None]), axis=0)
        return top, exponential, jnp.sum(blocks[:, 2:3, :], axis=0)

    line = lax.broadcasted_iota(jnp.int32, (8, T), 0)

    def packed_merge(blocks):
        top, exponential, picked = merge(blocks)
        return jnp.where(line == 0, top, jnp.where(line == 1, exponential, picked))

    for stage, axis in enumerate("zyx"):
        arrive(send(axis, lambda at: stat_recv.at[stage, 0], lambda d: stat_recv.at[stage, d]))
        merged = packed_merge(stat_recv[stage])
        if stage < 2:
            stat_recv[stage + 1, 0] = merged
    stat_all[core] = merged
    arrive(spread("core", stat_all.at[core]))
    logprob = []
    for m in range(2):
        top, exponential, picked = stat_all[m, 0:1], stat_all[m, 1:2], stat_all[m, 2:3]
        logprob.append(picked - (top + jnp.log(exponential)))
    difference = logprob[0] - logprob[1]
    hit = line == k_segment
    sums = jnp.sum(jnp.where(hit, difference, 0.0), axis=1, keepdims=True)
    length = jnp.sum(jnp.where(hit, 1.0, 0.0), axis=1, keepdims=True)
    square8 = lax.broadcasted_iota(jnp.int32, (8, 8), 0) == lax.broadcasted_iota(jnp.int32, (8, 8), 1)
    out[...] = jnp.sum(jnp.where(square8, sums / length, 0.0), axis=0, keepdims=True)

    flush(len(pending))


def per_device(
    residual, attn_gain, w_query, w_key, w_value, w_out, mlp_gain, w_gate, w_up, w_down, final_gain, w_head,
    seq_lengths, targets,
):
    anywhere = pl.BlockSpec(memory_space=pl.ANY)
    vmem = pl.BlockSpec(memory_space=pltpu.VMEM)
    smem = pl.BlockSpec(memory_space=pltpu.SMEM)
    dma = pltpu.SemaphoreType.DMA
    result = pl.pallas_call(
        kernel,
        out_shape=jax.ShapeDtypeStruct((1, SEQS), F32),
        in_specs=[anywhere] * 12 + [smem, anywhere],
        out_specs=vmem,
        scratch_shapes=[
            pltpu.VMEM((1, T), jnp.int32),
            pltpu.VMEM((2, 32, FEAT), BF16),
            pltpu.VMEM((7, 4, 8, HEAD), F32),
            pltpu.VMEM((4, 2, 32, FEAT), BF16),
            pltpu.VMEM((FEAT, QKV), BF16),
            pltpu.VMEM((CHIP, QW), BF16),
            pltpu.VMEM((CHIP, FF), BF16),
            pltpu.VMEM((CHIP, FF), BF16),
            pltpu.VMEM((CHIP, FF), BF16),
            pltpu.VMEM((2, D, VOCAB), BF16),
            pltpu.VMEM((FEAT,), F32),
            pltpu.VMEM((FEAT,), F32),
            pltpu.VMEM((FEAT,), F32),
            pltpu.VMEM((2, 1, FEAT), F32),
            pltpu.VMEM((2, 1, FEAT), F32),
            pltpu.VMEM((4, 2, 2, 16, QKV), F32),
            pltpu.VMEM((4, 2, 16, QKV), F32),
            pltpu.VMEM((4, 2, 16, QKV), F32),
            pltpu.VMEM((4, 2, 16, QKV), F32),
            pltpu.VMEM((2, 16, QKV), F32),
            pltpu.VMEM((16, QKV), F32),
            pltpu.VMEM((4, 2, 2, 16, QKV), BF16),
            pltpu.VMEM((T // 2, QW), BF16),
            pltpu.VMEM((4, 2, 16, CHIP), F32),
            pltpu.VMEM((4, 2, 16, CHIP), F32),
            pltpu.VMEM((2, 16, CHIP), F32),
            pltpu.VMEM((16, CHIP), F32),
            pltpu.VMEM((2, 16, CHIP), BF16),
            pltpu.VMEM((4, 2, 2, 16, CHIP), BF16),
            pltpu.VMEM((2, 4, 2, 32, FFP), F32),
            pltpu.VMEM((2, 4, 2, 32, FFP), BF16),
            pltpu.VMEM((4, 32, FFP), BF16),
            pltpu.VMEM((4, 32, FFP), BF16),
            pltpu.VMEM((32, FFP), BF16),
            pltpu.VMEM((4, 2, 32, FFP), BF16),
            pltpu.VMEM((4, 32, FFP), F32),
            pltpu.VMEM((4, 32, FFP), BF16),
            pltpu.VMEM((2, 32, FFP), F32),
            pltpu.VMEM((32, FFP), BF16),
            pltpu.VMEM((4, 2, 32, FFP), BF16),
            pltpu.VMEM((4, 2, 32, CHIP), F32),
            pltpu.VMEM((4, 2, 32, CHIP), F32),
            pltpu.VMEM((2, 32, CHIP), F32),
            pltpu.VMEM((32, CHIP), F32),
            pltpu.VMEM((4, 2, 4, 2, 32, 256), BF16),
            pltpu.VMEM((4, 2, 4, 2, 32, 256), BF16),
            pltpu.VMEM((4, 2, 4, 2, 32, HEAD), BF16),
            pltpu.VMEM((2, T, VOCAB), F32),
            pltpu.VMEM((3, 4, 8, T), F32),
            pltpu.VMEM((2, 8, T), F32),
            dma((13,)), dma((160,)), dma((160,)),
        ],
        compiler_params=pltpu.CompilerParams(
            collective_id=0, has_side_effects=True, vmem_limit_bytes=60 * 1024 * 1024
        ),
    )(
        residual, attn_gain, w_query, w_key, w_value, w_out.T, mlp_gain, w_gate, w_up,
        jnp.swapaxes(w_down, 1, 2), final_gain, w_head, seq_lengths, targets.reshape(1, T),
    )
    return result.reshape(SEQS)


def solution(mesh):
    placed = (
        P("row", "col"), P("col"), P("col", "row"), P("col", "row"), P("col", "row"), P("row", "col"), P("col"),
        P(None, "col", "row"), P(None, "col", "row"), P(None, "row", "col"), P("col"), P(None, ("row", "col")), P(), P(),
    )
    return jax.shard_map(per_device, mesh=mesh, in_specs=placed, out_specs=P(), check_vma=False)
```

time: 139 us -> 160 us (1.15)
  Pallas kernels: 138 us -> 159 us
    pallas_call x1, Pallas kernels: 138 us -> 159 us  [per_device(): pl.pallas_call(kernel, out_shape=jax.ShapeDtypeStruct((1, SEQS), F32), in...]
where the time goes in v6:
time: 160 us
  Pallas kernels  159 us (99%)
    pallas_call x1, Pallas kernels, per_device(): pl.pallas_call(kernel, out_shape=jax.ShapeDtypeStruct((1, SEQS), F32), in...  159 us

profile of v6, /device:TPU:1, one launch (start us, length us, event | category | flops | bytes accessed | tf_op | source)
XLA Modules:
  0.0 159.7 jit_solution(12935058249493113027)
XLA Ops:
  0.0 158.5 %shard_map.136 = f32[1,8]{1,0:T(1,128)} custom-call(bf16[32,320]{1,0:T(8,128)(2,1)} %res.1, f32[320]{0:T(512)} %attn_gain.1, bf16[320,640]{1,0:T(8,128)(2,1)} %w_query.1, bf16[320,128]{1,0:T(8,128)(2,1)} %w_key.1, bf16[320,128]{1,0:T(8,128)(2,1)} %w_value.1, bf16[320,640]{1,0:T(8,128)(2,1)} %bitcast.5, f32[320]{0:T(512)} %mlp_gain.1, ...), custom_call_target="tpu_custom_call" | custom-call | tf_op jit(solution)/shard_map/pallas_call | solution.py:429
  158.5 1.2 copy.16

commit v7 on v5

--- a/solution.py
+++ b/solution.py
@@ -64,6 +64,16 @@
     return jnp.sum(jnp.where(diagonal_of(count), rows[0:1], 0.0), axis=1, keepdims=True)
 
 
+def split_sum(total, width):
+    high = total.astype(BF16)
+    low = (total - high.astype(F32)).astype(BF16)
+    shape = (total.shape[0], width)
+    return (
+        jnp.broadcast_to(high.astype(F32), shape).astype(BF16),
+        jnp.broadcast_to(low.astype(F32), shape).astype(BF16),
+    )
+
+
 def inverse_rms(total):
     return lax.rsqrt(total / D + EPSILON)
 
@@ -82,11 +92,11 @@
 
 
 def kernel(
-    res, attn_gain, w_query, w_key, w_value, w_out, mlp_gain, w_gate, w_up, w_down, final_gain, w_head, lens, targets,
+    res, attn_gain, w_query, w_key, w_value, w_out, mlp_gain, w_gate, w_up, w_down, final_gain, w_head, lengths, targets,
     out,
-    target_row, res_chip, square_all, x_all, wqkv, wo, wg, wu, wd, wh, gain_a, gain_m, gain_f, mg, fg,
+    lens, target_row, res_chip, square_all, x_all, wqkv, wo, wg, wu, wd, wh, gain_a, gain_m, gain_f, mg, fg,
     part_own, part_pair, part_send, part_recv, qkv_all, attended, proj_send, proj_recv, stream_chip, norm_all, mlp_all,
-    gu_own, gu_send, gu_z0, gu_y0, gu_z1, gu_y1, mid_own, mid_send, mid2_own, mid2_send, hidden_all, down_send, down_recv,
+    gu_own, gu_send, gu_z0, gu_y0, gu_z1, gu_y1, mid_own, mid_send, mid2_own, hidden_all, down_send, down_recv,
     fin_a, fin_b, fin_c, logits, stat_send, stat_recv, stat2_recv,
     local_sem, swap_send, swap_recv, sq_s, sq_r, x_s, x_r, pair_s, pair_r, part_s, part_r, qkv_s, qkv_r, proj_s, proj_r,
     norm_s, norm_r, stream_s, stream_r, y_s, y_r, z_s, z_r, down_s, down_r, fin_s, fin_r, st_s, st_r, st2_s, st2_r,
@@ -148,6 +158,7 @@
 
     own("residual", res, res_chip.at[core])
     own("targets", targets, target_row)
+    own("lens", lengths, lens)
     own("gains", attn_gain, gain_a)
     own("gains", mlp_gain, gain_m)
     own("gains", final_gain, gain_f)
@@ -166,11 +177,10 @@
     cross_z = lax.rem(cz + 1 + 2 * (1 - zl), 4)
     cross_row, cross_col = at_xyz(cx, cy, cross_z)
     greet(cross_row, cross_col)
-    pl.semaphore_wait(barrier, 2 * (ROWS - 1) + (COLS - 1) + 1)
-
     ready("residual", "gains")
     x = res_chip[core].astype(F32)
     square_all[0] = to_row(jnp.sum(x * x, axis=1, keepdims=True))
+    pl.semaphore_wait(barrier, 2 * (ROWS - 1) + (COLS - 1) + 1)
 
     def sq_copy(d):
         return remote(square_all.at[0], square_all.at[d], sq_s.at[d], sq_r.at[d], row, col_at(d))
@@ -179,6 +189,7 @@
     mg[core] = gain_m[...].reshape(1, FEAT)
     fg[core] = gain_f[...].reshape(1, FEAT)
 
+    ready("lens")
     own_token = COLS * col + lax.broadcasted_iota(jnp.int32, (16, HEAD), 0)
     position = layout_of(lens, own_token)[1].astype(F32)
     lane = lax.broadcasted_iota(jnp.int32, (16, HEAD), 1)
@@ -282,23 +293,23 @@
     stream_chip[core] = stream
     stream = stream.astype(F32)
 
-    def norm(i, value, gain):
+    def norm(value, gain):
         count = value.shape[0]
-        norm_all[i, 0] = to_row(jnp.sum(value * value, axis=1, keepdims=True))
+        norm_all[0] = to_row(jnp.sum(value * value, axis=1, keepdims=True))
 
         def copy(d):
             return remote(
-                norm_all.at[i, 0], norm_all.at[i, d], norm_s.at[i, d], norm_r.at[i, d], row, chip_at(d) * 2 + core
+                norm_all.at[0], norm_all.at[d], norm_s.at[d], norm_r.at[d], row, chip_at(d) * 2 + core
             )
 
         start(1, CHIPS, copy)
         arrive(1, CHIPS, copy)
-        square = to_column(jnp.sum(norm_all[i], axis=0), count)
+        square = to_column(jnp.sum(norm_all[...], axis=0), count)
         gain = jnp.concatenate([gain[0], gain[1]], axis=1)
         return (value * inverse_rms(square) * gain).astype(BF16)
 
     ready("gains_pair")
-    mlp_all[row, core] = norm(0, stream, mg)
+    mlp_all[row, core] = norm(stream, mg)
 
     own_stream = mlp_all.at[row, core]
 
@@ -366,8 +377,7 @@
     arrive(1, 4, sum_y1)
     gu_y1[0] = jnp.zeros((2, 32, FFP), BF16)
     mid2_own[...] = gu_own[1, cy] + jnp.sum(gu_y1[...].astype(F32), axis=0)
-    mid2_send[...] = mid2_own[1 - zl].astype(BF16)
-    sum_z1 = to_z(mid2_send, gu_z1, 1)
+    sum_z1 = to_z(mid2_own.at[1 - zl], gu_z1, 1)
     start(0, 1, sum_z1)
 
     def activate(i, total):
@@ -387,7 +397,7 @@
     hid_z0 = to_z(own0, own0, 2)
     start(0, 1, hid_z0)
     arrive(0, 1, sum_z1)
-    activate(1, mid2_own[zl] + gu_z1[...].astype(F32))
+    activate(1, mid2_own[zl] + gu_z1[...])
     own1 = hidden_all.at[cy, zl, :, lanes(1)]
     hid_y1 = to_y(lambda y: own1, lambda d: own1, 2)
     start(1, 4, hid_y1)
@@ -417,11 +427,14 @@
     arrive(1, ROWS, down_copy)
     ready("stream_pair")
     final = stream_chip[...].reshape(32, CHIP).astype(F32) + jnp.sum(down_recv[...], axis=0)
-    final = norm(1, final, fg)
+    square_hi, square_lo = split_sum(jnp.sum(final * final, axis=1, keepdims=True), 64)
+    final = (final * jnp.concatenate([fg[0], fg[1]], axis=1)).astype(BF16)
 
     fin_a[cy, zl, cx, zh] = final[:, 0:256]
     fin_b[cy, zl, cx, zh] = final[:, 256:512]
-    fin_c[cy, zl, cx, zh] = final[:, 512:640]
+    fin_c[cy, zl, cx, zh, :, 0:128] = final[:, 512:640]
+    fin_c[cy, zl, cx, zh, :, 128:192] = square_hi
+    fin_c[cy, zl, cx, zh, :, 192:256] = square_lo
 
     parts = (fin_a, fin_b, fin_c)
     orders = ("zyx", "xzy", "yxz")
@@ -464,15 +477,19 @@
         for copy in gathers[2][p]:
             copy.wait_recv()
 
+    square = jnp.zeros((T, 1), F32)
     for y in range(4):
         pieces = []
         for z in range(2):
-            pieces += [fin_a[y, z].reshape(T, 256), fin_b[y, z].reshape(T, 256), fin_c[y, z].reshape(T, HEAD)]
+            c = fin_c[y, z].reshape(T, 256)
+            square = square + c[:, 128:129].astype(F32) + c[:, 192:193].astype(F32)
+            pieces += [fin_a[y, z].reshape(T, 256), fin_b[y, z].reshape(T, 256), c[:, 0:128]]
         states = jnp.concatenate(pieces, axis=1)
         for j in range(2):
             product = jnp.dot(states, wh[j, y * 2 * CHIP:(y + 1) * 2 * CHIP], preferred_element_type=F32)
             logits[j] = product if y == 0 else logits[j] + product
-    both = [logits[j] for j in range(2)]
+    scale = inverse_rms(square)
+    both = [logits[j] * scale for j in range(2)]
     top = jnp.maximum(*[jnp.max(l, axis=1, keepdims=True) for l in both])
     exponential = sum(jnp.sum(jnp.exp(l - top), axis=1, keepdims=True) for l in both)
     picked = jnp.zeros((T, 1), F32)
@@ -544,14 +561,14 @@
 ):
     anywhere = pl.BlockSpec(memory_space=pl.ANY)
     vmem = pl.BlockSpec(memory_space=pltpu.VMEM)
-    smem = pl.BlockSpec(memory_space=pltpu.SMEM)
     dma = pltpu.SemaphoreType.DMA
     result = pl.pallas_call(
         kernel,
         out_shape=jax.ShapeDtypeStruct((1, SEQS), F32),
-        in_specs=[anywhere] * 12 + [smem, anywhere],
+        in_specs=[anywhere] * 12 + [anywhere, anywhere],
         out_specs=vmem,
         scratch_shapes=[
+            pltpu.SMEM((SEQS,), jnp.int32),
             pltpu.VMEM((1, T), jnp.int32),
             pltpu.VMEM((2, 32, FEAT), BF16),
             pltpu.VMEM((COLS, 8, HEAD), F32),
@@ -576,36 +593,35 @@
             pltpu.VMEM((ROWS, 16, CHIP), F32),
             pltpu.VMEM((ROWS, 16, CHIP), F32),
             pltpu.VMEM((2, 16, CHIP), BF16),
-            pltpu.VMEM((2, CHIPS, 8, HEAD), F32),
+            pltpu.VMEM((CHIPS, 8, HEAD), F32),
             pltpu.VMEM((ROWS, 2, 16, CHIP), BF16),
             pltpu.VMEM((2, 4, 2, 32, FFP), F32),
             pltpu.VMEM((2, 4, 2, 32, FFP), BF16),
             pltpu.VMEM((4, 32, FFP), BF16),
             pltpu.VMEM((4, 32, FFP), BF16),
-            pltpu.VMEM((32, FFP), BF16),
+            pltpu.VMEM((32, FFP), F32),
             pltpu.VMEM((4, 2, 32, FFP), BF16),
             pltpu.VMEM((4, 32, FFP), F32),
             pltpu.VMEM((4, 32, FFP), BF16),
             pltpu.VMEM((2, 32, FFP), F32),
-            pltpu.VMEM((32, FFP), BF16),
             pltpu.VMEM((4, 2, 32, FFP), BF16),
             pltpu.VMEM((ROWS, 32, CHIP), F32),
             pltpu.VMEM((ROWS, 32, CHIP), F32),
             pltpu.VMEM((4, 2, 4, 2, 32, 256), BF16),
             pltpu.VMEM((4, 2, 4, 2, 32, 256), BF16),
-            pltpu.VMEM((4, 2, 4, 2, 32, HEAD), BF16),
+            pltpu.VMEM((4, 2, 4, 2, 32, 256), BF16),
             pltpu.VMEM((2, T, VOCAB), F32),
             pltpu.VMEM((8, T), F32),
             pltpu.VMEM((2, 4, 8, T), F32),
             pltpu.VMEM((2, 4, 8, T), F32),
-            dma((13,)), dma((9,)), dma((9,)),
+            dma((14,)), dma((9,)), dma((9,)),
             dma((COLS,)), dma((COLS,)),
             dma((ROWS,)), dma((ROWS,)),
             dma, dma,
             dma((CHIPS,)), dma((CHIPS,)),
             dma((COLS,)), dma((COLS,)),
             dma((ROWS,)), dma((ROWS,)),
-            dma((2, CHIPS)), dma((2, CHIPS)),
+            dma((CHIPS,)), dma((CHIPS,)),
             dma((2 * ROWS,)), dma((2 * ROWS,)),
             dma((4, 4)), dma((4, 4)),
             dma((4,)), dma((4,)),

time: 139 us -> 138 us (level)
  no operation moved by 1% of the time
where the time goes in v7:
time: 138 us
  Pallas kernels  137 us (99%)
    pallas_call x1, Pallas kernels, per_device(): pl.pallas_call(kernel, out_shape=jax.ShapeDtypeStruct((1, SEQS), F32), in...  137 us

profile of v7, /device:TPU:1, one launch (start us, length us, event | category | flops | bytes accessed | tf_op | source)
XLA Modules:
  0.0 137.9 jit_solution(7667436396311047474)
XLA Ops:
  0.0 136.7 %shard_map.136 = f32[1,8]{1,0:T(1,128)} custom-call(bf16[32,320]{1,0:T(8,128)(2,1)} %res.1, f32[320]{0:T(512)} %attn_gain.1, bf16[320,640]{1,0:T(8,128)(2,1)} %w_query.1, bf16[320,128]{1,0:T(8,128)(2,1)} %w_key.1, bf16[320,128]{1,0:T(8,128)(2,1)} %w_value.1, bf16[320,640]{1,0:T(8,128)(2,1)} %bitcast.5, f32[320]{0:T(512)} %mlp_gain.1, ...), custom_call_target="tpu_custom_call" | custom-call | tf_op jit(solution)/shard_map/pallas_call | solution.py:565
  136.7 1.2 copy.16

commit v8 on v7

--- a/solution.py
+++ b/solution.py
@@ -95,11 +95,11 @@
     res, attn_gain, w_query, w_key, w_value, w_out, mlp_gain, w_gate, w_up, w_down, final_gain, w_head, lengths, targets,
     out,
     lens, target_row, res_chip, square_all, x_all, wqkv, wo, wg, wu, wd, wh, gain_a, gain_m, gain_f, mg, fg,
-    part_own, part_pair, part_send, part_recv, qkv_all, attended, proj_send, proj_recv, stream_chip, norm_all, mlp_all,
+    part_own, part_pair, part_send, part_recv, qkv_all, attended, proj_send, proj_recv, stream_all,
     gu_own, gu_send, gu_z0, gu_y0, gu_z1, gu_y1, mid_own, mid_send, mid2_own, hidden_all, down_send, down_recv,
     fin_a, fin_b, fin_c, logits, stat_send, stat_recv, stat2_recv,
     local_sem, swap_send, swap_recv, sq_s, sq_r, x_s, x_r, pair_s, pair_r, part_s, part_r, qkv_s, qkv_r, proj_s, proj_r,
-    norm_s, norm_r, stream_s, stream_r, y_s, y_r, z_s, z_r, down_s, down_r, fin_s, fin_r, st_s, st_r, st2_s, st2_r,
+    stream_s, stream_r, y_s, y_r, z_s, z_r, down_s, down_r, fin_s, fin_r, st_s, st_r, st2_s, st2_r,
 ):
     row, col = lax.axis_index("row"), lax.axis_index("col")
     core = lax.rem(col, 2)
@@ -289,29 +289,9 @@
     arrive(1, ROWS, proj_copy)
     half_rows = pl.ds(pl.multiple_of(core * 16, 16), 16)
     residual = jnp.concatenate([res_chip[0, half_rows, :], res_chip[1, half_rows, :]], axis=1).astype(F32)
-    stream = (residual + jnp.sum(proj_recv[...], axis=0)).astype(BF16)
-    stream_chip[core] = stream
-    stream = stream.astype(F32)
-
-    def norm(value, gain):
-        count = value.shape[0]
-        norm_all[0] = to_row(jnp.sum(value * value, axis=1, keepdims=True))
-
-        def copy(d):
-            return remote(
-                norm_all.at[0], norm_all.at[d], norm_s.at[d], norm_r.at[d], row, chip_at(d) * 2 + core
-            )
-
-        start(1, CHIPS, copy)
-        arrive(1, CHIPS, copy)
-        square = to_column(jnp.sum(norm_all[...], axis=0), count)
-        gain = jnp.concatenate([gain[0], gain[1]], axis=1)
-        return (value * inverse_rms(square) * gain).astype(BF16)
-
-    ready("gains_pair")
-    mlp_all[row, core] = norm(stream, mg)
-
-    own_stream = mlp_all.at[row, core]
+    stream_all[row, core] = (residual + jnp.sum(proj_recv[...], axis=0)).astype(BF16)
+
+    own_stream = stream_all.at[row, core]
 
     def stream_copy(d):
         return remote(own_stream, own_stream, stream_s.at[d], stream_r.at[d], row_at(d), col)
@@ -321,15 +301,18 @@
 
     start(1, ROWS, stream_copy)
     start(0, ROWS, stream_cross)
-    swap("stream_pair", stream_chip.at[core], stream_chip.at[core])
     own("wh", w_head, wh.at[core])
     swap("wh", w_head, wh.at[core])
     wh_at = len(pending) - 1
-    ready("wg", "wu")
+    ready("wg", "wu", "gains_pair")
     arrive(1, ROWS, stream_copy)
     arrive(0, ROWS, stream_cross)
 
-    mlp_in = mlp_all[...].reshape(T, CHIP)
+    stream = stream_all[...].reshape(T, CHIP).astype(F32)
+    square_hi, square_lo = split_sum(jnp.sum(stream * stream, axis=1, keepdims=True), HALF - CHUNKS[0][1])
+    stream = stream * jnp.concatenate([mg[0], mg[1]], axis=1)
+    mlp_hi = stream.astype(BF16)
+    mlp_lo = (stream - mlp_hi.astype(F32)).astype(BF16)
 
     def y_peer(d):
         return (lax.rem(cy + d, 4) * 2 + zl) * 2 + core
@@ -348,14 +331,15 @@
     def gate_up(i):
         low, width = CHUNKS[i]
         for half, weight in enumerate((wg, wu)):
-            product = jnp.dot(mlp_in, weight[:, low:low + width], preferred_element_type=F32)
+            product = jnp.dot(mlp_hi, weight[:, low:low + width], preferred_element_type=F32)
+            product += jnp.dot(mlp_lo, weight[:, low:low + width], preferred_element_type=F32)
             product = product.reshape(4, 2, 32, width)
             gu_own[i, :, :, :, half * HALF:half * HALF + width] = product
             gu_send[i, :, :, :, half * HALF:half * HALF + width] = product.astype(BF16)
             if width < HALF:
-                rest = jnp.zeros((4, 2, 32, HALF - width), F32)
-                gu_own[i, :, :, :, half * HALF + width:(half + 1) * HALF] = rest
-                gu_send[i, :, :, :, half * HALF + width:(half + 1) * HALF] = rest.astype(BF16)
+                rest = (square_hi, square_lo)[half].reshape(4, 2, 32, HALF - width)
+                gu_own[i, :, :, :, half * HALF + width:(half + 1) * HALF] = rest.astype(F32)
+                gu_send[i, :, :, :, half * HALF + width:(half + 1) * HALF] = rest
 
     gate_up(0)
     sum_z0 = to_z(gu_send.at[0, :, 1 - zl], gu_z0, 0)
@@ -370,8 +354,15 @@
     pending.extend([wh_swap] + held)
 
     arrive(0, 1, sum_z0)
-    mid_own[...] = gu_own[0, :, zl] + gu_z0[...].astype(F32)
-    mid_send[...] = mid_own[...].astype(BF16)
+    middle = gu_own[0, :, zl] + gu_z0[...].astype(F32)
+    mid_own[...] = middle
+    mid_send[...] = middle.astype(BF16)
+    width = CHUNKS[0][1]
+    square = middle[:, :, width:width + 1] + middle[:, :, HALF + width:HALF + width + 1]
+    for half, rest in enumerate(split_sum(square.reshape(HEAD, 1), HALF - width)):
+        rest = rest.reshape(4, 32, HALF - width)
+        mid_own[:, :, half * HALF + width:(half + 1) * HALF] = rest.astype(F32)
+        mid_send[:, :, half * HALF + width:(half + 1) * HALF] = rest
     sum_y0 = to_y(lambda y: mid_send.at[y], lambda d: gu_y0.at[d], 1)
     start(1, 4, sum_y0)
     arrive(1, 4, sum_y1)
@@ -380,10 +371,10 @@
     sum_z1 = to_z(mid2_own.at[1 - zl], gu_z1, 1)
     start(0, 1, sum_z1)
 
-    def activate(i, total):
+    def activate(i, total, scale):
         low, width = CHUNKS[i]
-        gate = total[:, 0:width]
-        hidden = gate / (1.0 + jnp.exp(-gate)) * total[:, HALF:HALF + width]
+        gate = total[:, 0:width] * scale
+        hidden = gate / (1.0 + jnp.exp(-gate)) * (total[:, HALF:HALF + width] * scale)
         hidden_all[cy, zl, :, low:low + width] = hidden.astype(BF16)
 
     def lanes(i):
@@ -392,12 +383,14 @@
     hidden_all[cy, zl, :, FF:FFP] = jnp.zeros((32, FFP - FF), BF16)
     arrive(1, 4, sum_y0)
     gu_y0[0] = jnp.zeros((32, FFP), BF16)
-    activate(0, mid_own[cy] + jnp.sum(gu_y0[...].astype(F32), axis=0))
+    total = mid_own[cy] + jnp.sum(gu_y0[...].astype(F32), axis=0)
+    scale = inverse_rms(total[:, width:width + 1] + total[:, HALF + width:HALF + width + 1])
+    activate(0, total, scale)
     own0 = hidden_all.at[cy, zl, :, lanes(0)]
     hid_z0 = to_z(own0, own0, 2)
     start(0, 1, hid_z0)
     arrive(0, 1, sum_z1)
-    activate(1, mid2_own[zl] + gu_z1[...])
+    activate(1, mid2_own[zl] + gu_z1[...], scale)
     own1 = hidden_all.at[cy, zl, :, lanes(1)]
     hid_y1 = to_y(lambda y: own1, lambda d: own1, 2)
     start(1, 4, hid_y1)
@@ -425,8 +418,7 @@
     start(1, ROWS, down_copy)
     down_recv[0] = down_send[row]
     arrive(1, ROWS, down_copy)
-    ready("stream_pair")
-    final = stream_chip[...].reshape(32, CHIP).astype(F32) + jnp.sum(down_recv[...], axis=0)
+    final = stream_all[row].reshape(32, CHIP).astype(F32) + jnp.sum(down_recv[...], axis=0)
     square_hi, square_lo = split_sum(jnp.sum(final * final, axis=1, keepdims=True), 64)
     final = (final * jnp.concatenate([fg[0], fg[1]], axis=1)).astype(BF16)
 
@@ -592,8 +584,6 @@
             pltpu.VMEM((T // 2, QW), BF16),
             pltpu.VMEM((ROWS, 16, CHIP), F32),
             pltpu.VMEM((ROWS, 16, CHIP), F32),
-            pltpu.VMEM((2, 16, CHIP), BF16),
-            pltpu.VMEM((CHIPS, 8, HEAD), F32),
             pltpu.VMEM((ROWS, 2, 16, CHIP), BF16),
             pltpu.VMEM((2, 4, 2, 32, FFP), F32),
             pltpu.VMEM((2, 4, 2, 32, FFP), BF16),
@@ -614,14 +604,13 @@
             pltpu.VMEM((8, T), F32),
             pltpu.VMEM((2, 4, 8, T), F32),
             pltpu.VMEM((2, 4, 8, T), F32),
-            dma((14,)), dma((9,)), dma((9,)),
+            dma((14,)), dma((8,)), dma((8,)),
             dma((COLS,)), dma((COLS,)),
             dma((ROWS,)), dma((ROWS,)),
             dma, dma,
             dma((CHIPS,)), dma((CHIPS,)),
             dma((COLS,)), dma((COLS,)),
             dma((ROWS,)), dma((ROWS,)),
-            dma((CHIPS,)), dma((CHIPS,)),
             dma((2 * ROWS,)), dma((2 * ROWS,)),
             dma((4, 4)), dma((4, 4)),
             dma((4,)), dma((4,)),

time: 138 us -> 135 us (0.978)
  Pallas kernels: 137 us -> 133 us
    pallas_call x1, Pallas kernels: 137 us -> 133 us  [per_device(): pl.pallas_call(kernel, out_shape=jax.ShapeDtypeStruct((1, SEQS), F32), in...]
where the time goes in v8:
time: 135 us
  Pallas kernels  133 us (99%)
    pallas_call x1, Pallas kernels, per_device(): pl.pallas_call(kernel, out_shape=jax.ShapeDtypeStruct((1, SEQS), F32), in...  133 us

profile of v8, /device:TPU:1, one launch (start us, length us, event | category | flops | bytes accessed | tf_op | source)
XLA Modules:
  0.0 134.5 jit_solution(12532920831981325529)
XLA Ops:
  0.0 133.3 %shard_map.136 = f32[1,8]{1,0:T(1,128)} custom-call(bf16[32,320]{1,0:T(8,128)(2,1)} %res.1, f32[320]{0:T(512)} %attn_gain.1, bf16[320,640]{1,0:T(8,128)(2,1)} %w_query.1, bf16[320,128]{1,0:T(8,128)(2,1)} %w_key.1, bf16[320,128]{1,0:T(8,128)(2,1)} %w_value.1, bf16[320,640]{1,0:T(8,128)(2,1)} %bitcast.5, f32[320]{0:T(512)} %mlp_gain.1, ...), custom_call_target="tpu_custom_call" | custom-call | tf_op jit(solution)/shard_map/pallas_call | solution.py:557
  133.3 1.2 copy.16

commit v9 on v8

--- a/solution.py
+++ b/solution.py
@@ -328,7 +328,7 @@
     def to_z(src, dst, i):
         return lambda d: remote(src, dst, z_s.at[i], z_r.at[i], row, z_peer)
 
-    def gate_up(i):
+    def gate_up(i, leave):
         low, width = CHUNKS[i]
         for half, weight in enumerate((wg, wu)):
             product = jnp.dot(mlp_hi, weight[:, low:low + width], preferred_element_type=F32)
@@ -340,20 +340,29 @@
                 rest = (square_hi, square_lo)[half].reshape(4, 2, 32, HALF - width)
                 gu_own[i, :, :, :, half * HALF + width:(half + 1) * HALF] = rest.astype(F32)
                 gu_send[i, :, :, :, half * HALF + width:(half + 1) * HALF] = rest
-
-    gate_up(0)
-    sum_z0 = to_z(gu_send.at[0, :, 1 - zl], gu_z0, 0)
-    start(0, 1, sum_z0)
-    gate_up(1)
-    sum_y1 = to_y(lambda y: gu_send.at[1, y], lambda d: gu_y1.at[d], 0)
-    start(1, 4, sum_y1)
-    held = pending[-2:]
-    del pending[-2:]
+            leave(half)
+
+    def half_lanes(half):
+        return pl.ds(half * HALF, HALF)
+
+    def sum_z0(half):
+        part = half_lanes(half)
+        return to_z(gu_send.at[0, :, 1 - zl, :, part], gu_z0.at[:, :, part], 4 * half)
+
+    def sum_y1(half):
+        part = half_lanes(half)
+        return to_y(lambda y: gu_send.at[1, y, :, :, part], lambda d: gu_y1.at[d, :, :, part], 4 * half)
+
+    gate_up(0, lambda half: start(0, 1, sum_z0(half)))
+    gate_up(1, lambda half: start(1, 4, sum_y1(half)))
+    held = pending[-4:]
+    del pending[-4:]
     wh_swap = pending.pop(wh_at)
     flush()
     pending.extend([wh_swap] + held)
 
-    arrive(0, 1, sum_z0)
+    for half in range(2):
+        arrive(0, 1, sum_z0(half))
     middle = gu_own[0, :, zl] + gu_z0[...].astype(F32)
     mid_own[...] = middle
     mid_send[...] = middle.astype(BF16)
@@ -365,7 +374,8 @@
         mid_send[:, :, half * HALF + width:(half + 1) * HALF] = rest
     sum_y0 = to_y(lambda y: mid_send.at[y], lambda d: gu_y0.at[d], 1)
     start(1, 4, sum_y0)
-    arrive(1, 4, sum_y1)
+    for half in range(2):
+        arrive(1, 4, sum_y1(half))
     gu_y1[0] = jnp.zeros((2, 32, FFP), BF16)
     mid2_own[...] = gu_own[1, cy] + jnp.sum(gu_y1[...].astype(F32), axis=0)
     sum_z1 = to_z(mid2_own.at[1 - zl], gu_z1, 1)
@@ -491,7 +501,7 @@
         picked = picked + jnp.sum(jnp.where(ids == target, both[j], 0.0), axis=1, keepdims=True)
     lane = lax.broadcasted_iota(jnp.int32, (T, HEAD), 1)
     packed = jnp.where(lane == 0, top, jnp.where(lane == 1, exponential, picked))
-    stat_recv[0, 0] = jnp.transpose(packed)[0:8, :]
+    stat_recv[0] = jnp.transpose(packed)[0:8, :]
 
     def merge(blocks):
         top = jnp.max(blocks[:, 0:1, :], axis=0)
@@ -504,35 +514,25 @@
         top, exponential, picked = merge(blocks)
         return jnp.where(line == 0, top, jnp.where(line == 1, exponential, picked))
 
-    for stage in range(2):
-        def st_copy(d):
-            if stage == 0:
-                r, c = at_xyz(cx, cy, lax.rem(cz + d, 4))
-            else:
-                r, c = at_xyz(cx, lax.rem(cy + d, 4), cz)
-            return remote(stat_recv.at[stage, 0], stat_recv.at[stage, d], st_s.at[stage, d], st_r.at[stage, d], r, c)
-
-        each(1, 4, lambda d: st_copy(d).start())
-        arrive(1, 4, st_copy)
-        each(1, 4, lambda d: st_copy(d).wait_send())
-        merged = packed_merge(stat_recv[stage])
-        if stage == 0:
-            stat_recv[1, 0] = merged
-        else:
-            stat_send[...] = merged
-            stat2_recv[core, cx] = merged
-    own_stat = stat2_recv.at[core, cx]
+    def st_copy(d):
+        return remote(stat_recv.at[0], stat_recv.at[d], st_s.at[d], st_r.at[d], row, chip_at(d) * 2 + core)
+
+    start(1, CHIPS, st_copy)
+    arrive(1, CHIPS, st_copy)
+    stat_send[...] = packed_merge(stat_recv[...])
+    own_stat = stat2_recv.at[core, row]
 
     def st2_copy(d):
-        return remote(stat_send, own_stat, st2_s.at[d], st2_r.at[d], lax.rem(cx + d, 4) * 2 + zh, col)
+        return remote(stat_send, own_stat, st2_s.at[d], st2_r.at[d], row_at(d), col)
 
     def st2_cross(d):
-        return remote(stat_send, own_stat, st2_s.at[4 + d], st2_r.at[4 + d], lax.rem(cx + d, 4) * 2 + zh, sib)
-
-    start(1, 4, st2_copy)
-    start(0, 4, st2_cross)
-    arrive(1, 4, st2_copy)
-    arrive(0, 4, st2_cross)
+        return remote(stat_send, own_stat, st2_s.at[ROWS + d], st2_r.at[ROWS + d], row_at(d), sib)
+
+    start(1, ROWS, st2_copy)
+    start(0, ROWS, st2_cross)
+    stat2_recv[core, row] = stat_send[...]
+    arrive(1, ROWS, st2_copy)
+    arrive(0, ROWS, st2_cross)
     logprob = []
     for m in range(2):
         top, exponential, picked = merge(stat2_recv[m])
@@ -602,8 +602,8 @@
             pltpu.VMEM((4, 2, 4, 2, 32, 256), BF16),
             pltpu.VMEM((2, T, VOCAB), F32),
             pltpu.VMEM((8, T), F32),
-            pltpu.VMEM((2, 4, 8, T), F32),
-            pltpu.VMEM((2, 4, 8, T), F32),
+            pltpu.VMEM((CHIPS, 8, T), F32),
+            pltpu.VMEM((2, ROWS, 8, T), F32),
             dma((14,)), dma((8,)), dma((8,)),
             dma((COLS,)), dma((COLS,)),
             dma((ROWS,)), dma((ROWS,)),
@@ -612,12 +612,12 @@
             dma((COLS,)), dma((COLS,)),
             dma((ROWS,)), dma((ROWS,)),
             dma((2 * ROWS,)), dma((2 * ROWS,)),
-            dma((4, 4)), dma((4, 4)),
-            dma((4,)), dma((4,)),
+            dma((5, 4)), dma((5, 4)),
+            dma((5,)), dma((5,)),
             dma((ROWS,)), dma((ROWS,)),
             dma((54,)), dma((54,)),
-            dma((2, 4)), dma((2, 4)),
             dma((CHIPS,)), dma((CHIPS,)),
+            dma((2 * ROWS,)), dma((2 * ROWS,)),
         ],
         compiler_params=pltpu.CompilerParams(
             collective_id=0, has_side_effects=True, vmem_limit_bytes=60 * 1024 * 1024

time: 135 us -> 133 us (0.985)
  Pallas kernels: 133 us -> 131 us
    pallas_call x1, Pallas kernels: 133 us -> 131 us  [per_device(): pl.pallas_call(kernel, out_shape=jax.ShapeDtypeStruct((1, SEQS), F32), in...]
where the time goes in v9:
time: 133 us
  Pallas kernels  131 us (98%)
    pallas_call x1, Pallas kernels, per_device(): pl.pallas_call(kernel, out_shape=jax.ShapeDtypeStruct((1, SEQS), F32), in...  131 us

profile of v9, /device:TPU:1, one launch (start us, length us, event | category | flops | bytes accessed | tf_op | source)
XLA Modules:
  0.0 132.5 jit_solution(7094293162173866922)
XLA Ops:
  0.0 131.3 %shard_map.136 = f32[1,8]{1,0:T(1,128)} custom-call(bf16[32,320]{1,0:T(8,128)(2,1)} %res.1, f32[320]{0:T(512)} %attn_gain.1, bf16[320,640]{1,0:T(8,128)(2,1)} %w_query.1, bf16[320,128]{1,0:T(8,128)(2,1)} %w_key.1, bf16[320,128]{1,0:T(8,128)(2,1)} %w_value.1, bf16[320,640]{1,0:T(8,128)(2,1)} %bitcast.5, f32[320]{0:T(512)} %mlp_gain.1, ...), custom_call_target="tpu_custom_call" | custom-call | tf_op jit(solution)/shard_map/pallas_call | solution.py:557
  131.3 1.2 copy.16

commit v10 on v9

--- a/solution.py
+++ b/solution.py
@@ -99,7 +99,7 @@
     gu_own, gu_send, gu_z0, gu_y0, gu_z1, gu_y1, mid_own, mid_send, mid2_own, hidden_all, down_send, down_recv,
     fin_a, fin_b, fin_c, logits, stat_send, stat_recv, stat2_recv,
     local_sem, swap_send, swap_recv, sq_s, sq_r, x_s, x_r, pair_s, pair_r, part_s, part_r, qkv_s, qkv_r, proj_s, proj_r,
-    stream_s, stream_r, y_s, y_r, z_s, z_r, down_s, down_r, fin_s, fin_r, st_s, st_r, st2_s, st2_r,
+    stream_s, stream_r, y_s, y_r, z_s, z_r, hid_s, hid_r, down_s, down_r, fin_s, fin_r, st_s, st_r, st2_s, st2_r,
 ):
     row, col = lax.axis_index("row"), lax.axis_index("col")
     core = lax.rem(col, 2)
@@ -402,21 +402,20 @@
     arrive(0, 1, sum_z1)
     activate(1, mid2_own[zl] + gu_z1[...], scale)
     own1 = hidden_all.at[cy, zl, :, lanes(1)]
-    hid_y1 = to_y(lambda y: own1, lambda d: own1, 2)
-    start(1, 4, hid_y1)
+
+    def hid_1(d):
+        return remote(own1, own1, hid_s.at[d], hid_r.at[d], row, chip_at(d) * 2 + core)
+
+    start(1, CHIPS, hid_1)
     arrive(0, 1, hid_z0)
     both0 = hidden_all.at[cy, :, :, lanes(0)]
     hid_y0 = to_y(lambda y: both0, lambda d: both0, 3)
     start(1, 4, hid_y0)
-    arrive(1, 4, hid_y1)
-    four1 = hidden_all.at[:, zl, :, lanes(1)]
-    hid_z1 = to_z(four1, four1, 3)
-    start(0, 1, hid_z1)
     ready("wd")
 
     product = jnp.zeros((T, CHIP), F32)
     for i, (low, width) in enumerate(CHUNKS):
-        arrive(*((1, 4, hid_y0) if i == 0 else (0, 1, hid_z1)))
+        arrive(*((1, 4, hid_y0) if i == 0 else (1, CHIPS, hid_1)))
         hidden = hidden_all[:, :, :, low:low + width].reshape(T, width)
         product += dot_nt(hidden, wd[:, low:low + width])
     down_send[...] = product.reshape(ROWS, 32, CHIP)
@@ -614,6 +613,7 @@
             dma((2 * ROWS,)), dma((2 * ROWS,)),
             dma((5, 4)), dma((5, 4)),
             dma((5,)), dma((5,)),
+            dma((CHIPS,)), dma((CHIPS,)),
             dma((ROWS,)), dma((ROWS,)),
             dma((54,)), dma((54,)),
             dma((CHIPS,)), dma((CHIPS,)),

time: 133 us -> 134 us (level)
  no operation moved by 1% of the time
where the time goes in v10:
time: 134 us
  Pallas kernels  132 us (99%)
    pallas_call x1, Pallas kernels, per_device(): pl.pallas_call(kernel, out_shape=jax.ShapeDtypeStruct((1, SEQS), F32), in...  132 us

profile of v10, /device:TPU:1, one launch (start us, length us, event | category | flops | bytes accessed | tf_op | source)
XLA Modules:
  0.0 133.7 jit_solution(6418570358136349760)
XLA Ops:
  0.0 132.5 %shard_map.136 = f32[1,8]{1,0:T(1,128)} custom-call(bf16[32,320]{1,0:T(8,128)(2,1)} %res.1, f32[320]{0:T(512)} %attn_gain.1, bf16[320,640]{1,0:T(8,128)(2,1)} %w_query.1, bf16[320,128]{1,0:T(8,128)(2,1)} %w_key.1, bf16[320,128]{1,0:T(8,128)(2,1)} %w_value.1, bf16[320,640]{1,0:T(8,128)(2,1)} %bitcast.5, f32[320]{0:T(512)} %mlp_gain.1, ...), custom_call_target="tpu_custom_call" | custom-call | tf_op jit(solution)/shard_map/pallas_call | solution.py:556
  132.5 1.2 copy.16
